TPU v7x, 256 devices: a whole 4x4x8 slice. The times are simulated.
256 devices in a mesh: seq: 32 (over z, x_hi, core), kv: 8 (over x_lo, y).
Axes of the slice: x: 4 (x_hi: 2, x_lo: 2; x = x_hi * 2 + x_lo), y: 4, z: 8, core: 2. Of those that a mesh axis runs over, the one named last changes fastest.
Arguments:
- queries: bfloat16 [4096, 8192], P('seq', 'kv'), may hold values from -60 to 60
- keys: bfloat16 [4096, 1024], P('seq', 'kv'), may hold values from -8 to 8
- values: bfloat16 [4096, 1024], P('seq', 'kv'), may hold values from -6 to 6
- out_weight: bfloat16 [8192, 8192], P(None, ('kv', 'seq')), may hold values from -0.0625 to 0.0625
- out_grad: bfloat16 [4096, 8192], P('seq', 'kv'), may hold values from -6 to 6
- doc_ids: int32 [4096], P('seq'), may hold values from 0 to 6, never falling along the last dimension, each value on 1 to 1152 neighbouring positions
- block_mask: int32 [32, 32], P('seq'), may hold values 0 or 1
- positions: int32 [3, 4096], P(None, 'seq'), may hold values from 0 to 1023
Outputs:
- layer_out: bfloat16 [4096, 8192], P('seq', 'kv')
- query_grad: bfloat16 [4096, 8192], P('seq', 'kv')
- key_grad: bfloat16 [4096, 1024], P('seq', 'kv')
- value_grad: bfloat16 [4096, 1024], P('seq', 'kv')
Inputs may be any that keep to these rules, and one draw needn't show every extreme that they name: `doc_ids`: every document has at most 1152 tokens, and one has exactly 1152.
All inputs are finite; a program needn't handle non-finite values. No bound on the sum of `block_mask` on one device may be relied on, other than what follows from the above.
Results may differ from a plain program's by a relative error of at most 0.017.
Values may be sent and summed in bfloat16 or wider, within the bound.
A program may use at most 128 MiB of HBM per device.

v0:
```python
import math

import jax
import jax.numpy as jnp
from jax import lax
from jax.sharding import PartitionSpec as P

HD = 128
BLK = 128
REACH = 9


rope_base = 1000000.0


def shifted(block, axis, distance):
    devices = range(lax.axis_size(axis))
    route = [(i - distance, i) for i in devices if i - distance in devices]
    return lax.ppermute(block, axis, route)


def rope_tables(positions):
    pairs = HD // 2
    index = jnp.arange(pairs)
    inv_freq = jnp.exp(index.astype(jnp.float32) * (-2.0 * math.log(rope_base) / HD))
    temporal = HD // 8
    which = jnp.where(index >= pairs - temporal, 0, jnp.where(index % 2 == 0, 1, 2))
    places = positions.astype(jnp.float32)
    chosen = jnp.where((which == 0)[:, None], places[0][None, :], 0.0)
    chosen = chosen + jnp.where((which == 1)[:, None], places[1][None, :], 0.0)
    chosen = chosen + jnp.where((which == 2)[:, None], places[2][None, :], 0.0)
    angle = chosen.T * inv_freq[None, :]
    return (jnp.cos(angle), jnp.sin(angle))


def rotate(block, cosine, sine, sign):
    half = HD // 2
    first = block[..., :half]
    second = block[..., half:]
    cos_part = cosine[:, None, :]
    sin_part = sine[:, None, :] * sign
    return jnp.concatenate(
        [first * cos_part - second * sin_part, second * cos_part + first * sin_part], axis=-1
    )


def allowed_mask(shard, doc_query, doc_key, mask_rows):
    length = doc_query.shape[0]
    width = doc_key.shape[0]
    query_pos = shard * length + jnp.arange(length, dtype=jnp.int32)
    key_pos = (shard - REACH) * length + jnp.arange(width, dtype=jnp.int32)
    near = jnp.repeat(jnp.repeat(mask_rows, BLK, axis=0), BLK, axis=1) > 0
    same_block = query_pos[:, None] // BLK == key_pos[None, :] // BLK
    return (
        (doc_query[:, None] == doc_key[None, :])
        & (key_pos[None, :] <= query_pos[:, None])
        & (key_pos[None, :] >= 0)
        & (near | same_block)
    )


def attend(query, key_win, value_win, allowed, grad_out):
    scale = HD ** (-0.5)
    contract = (((1,), (1,)), ((), ()))
    columns = (((0,), (0,)), ((), ()))
    scores = lax.dot_general(query, key_win, contract, preferred_element_type=jnp.float32) * scale
    scores = jnp.where(allowed, scores, -1e30)
    top = jnp.max(scores, axis=1, keepdims=True)
    expo = jnp.exp(scores - top)
    weights = (expo / jnp.sum(expo, axis=1, keepdims=True)).astype(jnp.bfloat16)
    output = jnp.dot(weights, value_win, preferred_element_type=jnp.float32).astype(jnp.bfloat16)
    delta = jnp.sum(
        grad_out.astype(jnp.float32) * output.astype(jnp.float32), axis=1, keepdims=True
    )
    dprob = lax.dot_general(grad_out, value_win, contract, preferred_element_type=jnp.float32)
    dscore = (weights.astype(jnp.float32) * (dprob - delta)).astype(jnp.bfloat16)
    dquery = jnp.dot(dscore, key_win, preferred_element_type=jnp.float32) * scale
    dkey = lax.dot_general(dscore, query, columns, preferred_element_type=jnp.float32) * scale
    dvalue = lax.dot_general(weights, grad_out, columns, preferred_element_type=jnp.float32)
    return (output, dquery, dkey, dvalue)


def per_device(queries, keys, values, out_weight, out_grad, doc_ids, block_mask, positions):
    length = queries.shape[0]
    groups = keys.shape[1] // HD
    heads = queries.shape[1] // HD
    per_group = heads // groups
    kv_count = lax.axis_size("kv")
    seq_count = lax.axis_size("seq")
    shard = lax.axis_index("seq")
    contract = (((1,), (1,)), ((), ()))
    cosine, sine = rope_tables(positions)
    q_rot = (
        rotate(queries.astype(jnp.float32).reshape(length, heads, HD), cosine, sine, 1.0)
        .astype(jnp.bfloat16)
        .reshape(length, heads * HD)
    )
    k_rot = (
        rotate(keys.astype(jnp.float32).reshape(length, groups, HD), cosine, sine, 1.0)
        .astype(jnp.bfloat16)
        .reshape(length, groups * HD)
    )
    pieces = lax.all_to_all(out_weight, "kv", split_axis=0, concat_axis=1, tiled=True)
    stripes = lax.all_gather(pieces, "seq", axis=1, tiled=True)
    row_count = stripes.shape[0]
    row_weight = (
        stripes.reshape(row_count, seq_count, kv_count, -1)
        .transpose(0, 2, 1, 3)
        .reshape(row_count, -1)
    )
    head_grad = lax.dot_general(
        lax.all_gather(out_grad, "kv", axis=1, tiled=True),
        row_weight,
        contract,
        preferred_element_type=jnp.float32,
    ).astype(jnp.bfloat16)
    key_parts = []
    value_parts = []
    doc_parts = []
    for reach in range(REACH, 0, -1):
        moved = shifted((k_rot, values, doc_ids), "seq", reach)
        key_parts.append(moved[0])
        value_parts.append(moved[1])
        doc_parts.append(moved[2])
    key_win = jnp.concatenate(key_parts + [k_rot], axis=0)
    value_win = jnp.concatenate(value_parts + [values], axis=0)
    doc_win = jnp.concatenate(doc_parts + [doc_ids], axis=0)
    blocks_dev = length // BLK
    mask_pad = jnp.pad(block_mask, ((0, 0), (REACH * blocks_dev, 0)))
    mask_rows = lax.dynamic_slice_in_dim(mask_pad, shard * blocks_dev, (REACH + 1) * blocks_dev, 1)
    allowed = allowed_mask(shard, doc_ids, doc_win, mask_rows)
    window = key_win.shape[0]
    outputs = []
    dqueries = []
    dkey_sum = jnp.zeros((window, HD), jnp.float32)
    dvalue_sum = jnp.zeros((window, HD), jnp.float32)
    for inner in range(per_group):
        output, dquery, dkey, dvalue = attend(
            q_rot[:, inner * HD : (inner + 1) * HD],
            key_win,
            value_win,
            allowed,
            head_grad[:, inner * HD : (inner + 1) * HD],
        )
        outputs.append(output)
        dqueries.append(dquery)
        dkey_sum = dkey_sum + dkey
        dvalue_sum = dvalue_sum + dvalue
    attn = jnp.concatenate(outputs, axis=1)
    dq_rot = jnp.stack(dqueries, axis=1)
    out_terms = jnp.dot(attn, row_weight, preferred_element_type=jnp.float32)
    layer_out = lax.psum_scatter(
        out_terms.astype(jnp.bfloat16), "kv", scatter_dimension=1, tiled=True
    )
    own = REACH * length
    dk_total = dkey_sum[own:]
    dv_total = dvalue_sum[own:]
    for reach in range(1, REACH + 1):
        slot = (REACH - reach) * length
        back = (
            shifted(dkey_sum[slot : slot + length].astype(jnp.bfloat16), "seq", -reach).astype(
                jnp.float32
            ),
            shifted(dvalue_sum[slot : slot + length].astype(jnp.bfloat16), "seq", -reach).astype(
                jnp.float32
            ),
        )
        dk_total = dk_total + back[0]
        dv_total = dv_total + back[1]
    query_grad = rotate(dq_rot, cosine, sine, -1.0).astype(jnp.bfloat16).reshape(length, heads * HD)
    key_grad = (
        rotate(dk_total.reshape(length, groups, HD), cosine, sine, -1.0)
        .astype(jnp.bfloat16)
        .reshape(length, groups * HD)
    )
    value_grad = dv_total.astype(jnp.bfloat16)
    return (layer_out, query_grad, key_grad, value_grad)


def solution(mesh):
    in_specs = (
        P("seq", "kv"),
        P("seq", "kv"),
        P("seq", "kv"),
        P(None, ("kv", "seq")),
        P("seq", "kv"),
        P("seq"),
        P("seq", None),
        P(None, "seq"),
    )
    out_specs = (P("seq", "kv"), P("seq", "kv"), P("seq", "kv"), P("seq", "kv"))
    return jax.shard_map(
        per_device, mesh=mesh, in_specs=in_specs, out_specs=out_specs, check_vma=False
    )
```

profile of v0, /device:TPU:97, one launch (start us, length us, event | category | flops | bytes accessed | tf_op | source)
XLA Modules:
  0.0 326.5 jit_solution(11807126632714953691)
XLA Ops:
  8.3 13.7 %all_to_all.19 = bf16[8,1024,32]{1,2,0:T(8,128)(2,1)} all-to-all(bf16[8,1024,32]{1,2,0:T(8,128)(2,1)S(1)} %bitcast.142), channel_id=1, replica_groups=mesh['seq'=32,'kv'=8] {'kv'}, dimensions={0} | all-to-all | bytes 1048576 | tf_op jit(solution)/shard_map/all_to_all | solution.py:103
  23.9 9.7 %collective-permute-start.9 = (bf16[128,128]{0,1:T(8,128)(2,1)S(1)}, bf16[128,128]{0,1:T(8,128)(2,1)S(1)}, u32[]{:S(2)}, u32[]{:S(2)}) collective-permute-start(bf16[128,128]{0,1:T(8,128)(2,1)S(1)} %pad_maximum_fusion.2), channel_id=1, source_target_pairs={{0,72},{8,80},{16,88},{24,96},{32,104},{40,112},{48,120},{56,128},... | collective-permute-start | bytes 98312 | tf_op jit(solution)/shard_map/ppermute | solution.py:19
  33.6 3.1 collective-permute-start.10
  36.7 1.9 collective-permute-start.11
  38.6 2.2 collective-permute-start.12
  40.8 1.9 collective-permute-start
  45.8 2.7 collective-permute-done
  50.4 3.6 %collective-permute-done.1 = s32[128]{0:T(128)S(1)} collective-permute-done((s32[128]{0:T(128)}, s32[128]{0:T(128)S(1)}, u32[]{:S(2)}, u32[]{:S(2)}) %collective-permute-start.1) | collective-permute-done | bytes 544 | tf_op jit(solution)/shard_map/ppermute | solution.py:19
  54.0 6.3 %collective-permute-start.2 = (s32[128]{0:T(128)}, s32[128]{0:T(128)S(1)}, u32[]{:S(2)}, u32[]{:S(2)}) collective-permute-start(s32[128]{0:T(128)} %param.13), channel_id=1, source_target_pairs={{0,56},{8,64},{16,72},{24,80},{32,88},{40,96},{48,104},{56,112},{6... | collective-permute-start | bytes 1544 | tf_op jit(solution)/shard_map/ppermute | solution.py:19
  60.3 2.0 collective-permute-done.2
  62.3 4.8 %collective-permute-start.3 = (s32[128]{0:T(128)}, s32[128]{0:T(128)S(1)}, u32[]{:S(2)}, u32[]{:S(2)}) collective-permute-start(s32[128]{0:T(128)} %param.13), channel_id=1, source_target_pairs={{0,48},{8,56},{16,64},{24,72},{32,80},{40,88},{48,96},{56,104},{64... | collective-permute-start | bytes 1544 | tf_op jit(solution)/shard_map/ppermute | solution.py:19
  67.1 3.0 collective-permute-done.3
  70.1 6.7 %collective-permute-start.4 = (s32[128]{0:T(128)}, s32[128]{0:T(128)S(1)}, u32[]{:S(2)}, u32[]{:S(2)}) collective-permute-start(s32[128]{0:T(128)} %param.13), channel_id=1, source_target_pairs={{0,40},{8,48},{16,56},{24,64},{32,72},{40,80},{48,88},{56,96},{64,... | collective-permute-start | bytes 1544 | tf_op jit(solution)/shard_map/ppermute | solution.py:19
  77.6 5.6 %collective-permute-start.5 = (s32[128]{0:T(128)}, s32[128]{0:T(128)S(1)}, u32[]{:S(2)}, u32[]{:S(2)}) collective-permute-start(s32[128]{0:T(128)} %param.13), channel_id=1, source_target_pairs={{0,32},{8,40},{16,48},{24,56},{32,64},{40,72},{48,80},{56,88},{64,... | collective-permute-start | bytes 1544 | tf_op jit(solution)/shard_map/ppermute | solution.py:19
  84.1 10.3 %collective-permute-start.6 = (s32[128]{0:T(128)}, s32[128]{0:T(128)S(1)}, u32[]{:S(2)}, u32[]{:S(2)}) collective-permute-start(s32[128]{0:T(128)} %param.13), channel_id=1, source_target_pairs={{0,24},{8,32},{16,40},{24,48},{32,56},{40,64},{48,72},{56,80},{64,... | collective-permute-start | bytes 1544 | tf_op jit(solution)/shard_map/ppermute | solution.py:19
  95.2 2.7 collective-permute-start.7
  98.0 4.1 %collective-permute-done.7 = s32[128]{0:T(128)S(1)} collective-permute-done((s32[128]{0:T(128)}, s32[128]{0:T(128)S(1)}, u32[]{:S(2)}, u32[]{:S(2)}) %collective-permute-start.7) | collective-permute-done | bytes 544 | tf_op jit(solution)/shard_map/ppermute | solution.py:19
  102.1 4.8 %collective-permute-start.8 = (s32[128]{0:T(128)}, s32[128]{0:T(128)S(1)}, u32[]{:S(2)}, u32[]{:S(2)}) collective-permute-start(s32[128]{0:T(128)} %param.13), channel_id=1, source_target_pairs={{0,8},{8,16},{16,24},{24,32},{32,40},{40,48},{48,56},{56,64},{64,7... | collective-permute-start | bytes 1544 | tf_op jit(solution)/shard_map/ppermute | solution.py:19
  107.7 6.2 %collective-permute-start.13 = (bf16[128,128]{0,1:T(8,128)(2,1)S(1)}, bf16[128,128]{0,1:T(8,128)(2,1)S(1)}, u32[]{:S(2)}, u32[]{:S(2)}) collective-permute-start(bf16[128,128]{0,1:T(8,128)(2,1)S(1)} %pad_maximum_fusion.2), channel_id=1, source_target_pairs={{0,40},{8,48},{16,56},{24,64},{32,72},{40,80},{48,88},{56,96},{64,... | collective-permute-start | bytes 98312 | tf_op jit(solution)/shard_map/ppermute | solution.py:19
  114.6 1.9 collective-permute-start.14
  116.6 6.4 %collective-permute-start.15 = (bf16[128,128]{0,1:T(8,128)(2,1)S(1)}, bf16[128,128]{0,1:T(8,128)(2,1)S(1)}, u32[]{:S(2)}, u32[]{:S(2)}) collective-permute-start(bf16[128,128]{0,1:T(8,128)(2,1)S(1)} %pad_maximum_fusion.2), channel_id=1, source_target_pairs={{0,24},{8,32},{16,40},{24,48},{32,56},{40,64},{48,72},{56,80},{64,... | collective-permute-start | bytes 98312 | tf_op jit(solution)/shard_map/ppermute | solution.py:19
  123.1 1.9 collective-permute-start.16
  125.0 4.9 %collective-permute-start.17 = (bf16[128,128]{0,1:T(8,128)(2,1)S(1)}, bf16[128,128]{0,1:T(8,128)(2,1)S(1)}, u32[]{:S(2)}, u32[]{:S(2)}) collective-permute-start(bf16[128,128]{0,1:T(8,128)(2,1)S(1)} %pad_maximum_fusion.2), channel_id=1, source_target_pairs={{0,8},{8,16},{16,24},{24,32},{32,40},{40,48},{48,56},{56,64},{64,7... | collective-permute-start | bytes 98312 | tf_op jit(solution)/shard_map/ppermute | solution.py:19
  129.9 1.9 collective-permute-start.18
  131.9 1.9 collective-permute-start.19
  133.8 1.9 collective-permute-start.20
  135.8 1.9 collective-permute-start.21
  137.8 1.9 collective-permute-start.22
  149.2 1.9 collective-permute-start.23
  153.1 1.9 collective-permute-start.25
  155.0 2.1 collective-permute-start.26
  157.2 2.3 collective-permute-done.24
  171.3 14.3 %copy.33 = bf16[1024,8,32,32]{0,3,2,1:T(8,128)(2,1)} copy(bf16[1024,8,32,32]{0,3,1,2:T(8,128)(2,1)} %bitcast.139) | data formatting | bytes 33554432 | tf_op jit(solution)/shard_map/transpose | solution.py:108
  185.6 23.4 %all-gather.5.cloned.1.call-done = bf16[128,8192]{1,0:T(8,128)(2,1)} async-done(((bf16[128,1024]{1,0:T(8,128)(2,1)}), bf16[128,8192]{1,0:T(8,128)(2,1)}) %all-gather.5.cloned.1.call-update) | async-done | bytes 2097168 | tf_op jit(solution)/shard_map/all_gather | solution.py:112
  209.1 13.0 %convolution_convert_fusion.1 = bf16[128,1024]{0,1:T(8,128)(2,1)S(1)} fusion(bf16[128,8192]{1,0:T(8,128)(2,1)} %all-gather.5.cloned.1.call-done, bf16[1024,8192]{0,1:T(8,128)(2,1)} %bitcast.137), kind=kOutput, calls=%fused_computation.56 | convolution fusion | flops 2147614720 | bytes 19136512 | tf_op jit(solution)/shard_map/dot_general | solution.py:111
  231.6 13.1 %convolution_convert_fusion = bf16[128,8192]{1,0:T(8,128)(2,1)} fusion(bf16[128,1024]{0,1:T(8,128)(2,1)} %copy-done.6, bf16[1024,8192]{0,1:T(8,128)(2,1)} %bitcast.138), kind=kOutput, calls=%fused_computation | convolution fusion | flops 2148532224 | bytes 19136512 | tf_op jit(solution)/shard_map/dot_general | solution.py:151
  251.3 2.1 fusion.124
  254.0 7.9 %collective-permute-start.27 = (bf16[128,128]{0,1:T(8,128)(2,1)S(1)}, bf16[128,128]{0,1:T(8,128)(2,1)S(1)}, u32[]{:S(2)}, u32[]{:S(2)}) collective-permute-start(bf16[128,128]{0,1:T(8,128)(2,1)S(1)} %get-tuple-element.41), channel_id=1, source_target_pairs={{8,0},{16,8},{24,16},{32,24},{40,32},{48,40},{56,48},{64,56},{72,6... | collective-permute-start | bytes 98312 | tf_op jit(solution)/shard_map/ppermute | solution.py:19
  261.9 4.2 %collective-permute-start.28 = (bf16[128,128]{0,1:T(8,128)(2,1)S(1)}, bf16[128,128]{0,1:T(8,128)(2,1)S(1)}, u32[]{:S(2)}, u32[]{:S(2)}) collective-permute-start(bf16[128,128]{0,1:T(8,128)(2,1)S(1)} %get-tuple-element.49), channel_id=1, source_target_pairs={{16,0},{24,8},{32,16},{40,24},{48,32},{56,40},{64,48},{72,56},{80,... | collective-permute-start | bytes 98312 | tf_op jit(solution)/shard_map/ppermute | solution.py:19
  266.2 2.7 collective-permute-start.29
  268.8 2.1 collective-permute-start.30
  270.9 1.9 collective-permute-start.31
  277.6 4.0 %collective-permute-start.32 = (bf16[128,128]{0,1:T(8,128)(2,1)}, bf16[128,128]{0,1:T(8,128)(2,1)S(1)}, u32[]{:S(2)}, u32[]{:S(2)}) collective-permute-start(bf16[128,128]{0,1:T(8,128)(2,1)} %get-tuple-element.45), channel_id=1, source_target_pairs={{48,0},{56,8},{64,16},{72,24},{80,32},{88,40},{96,48},{104,56},{11... | collective-permute-start | bytes 98312 | tf_op jit(solution)/shard_map/ppermute | solution.py:19
  288.4 2.3 collective-permute-start.36
  292.6 3.8 %collective-permute-start.38 = (bf16[128,128]{1,0:T(8,128)(2,1)}, bf16[128,128]{1,0:T(8,128)(2,1)S(1)}, u32[]{:S(2)}, u32[]{:S(2)}) collective-permute-start(bf16[128,128]{1,0:T(8,128)(2,1)} %get-tuple-element.39), channel_id=1, source_target_pairs={{24,0},{32,8},{40,16},{48,24},{56,32},{64,40},{72,48},{80,56},{88,... | collective-permute-start | bytes 98312 | tf_op jit(solution)/shard_map/ppermute | solution.py:19
  306.0 1.9 collective-permute-start.43
  313.5 2.0 collective-permute-done.43
  315.5 3.8 %collective-permute-done.44 = bf16[128,128]{1,0:T(8,128)(2,1)S(1)} collective-permute-done((bf16[128,128]{1,0:T(8,128)(2,1)S(1)}, bf16[128,128]{1,0:T(8,128)(2,1)S(1)}, u32[]{:S(2)}, u32[]{:S(2)}) %collective-permute-start.44) | collective-permute-done | bytes 32800 | tf_op jit(solution)/shard_map/ppermute | solution.py:19
  (218 shorter events, 80.6 us)
Async XLA Ops:
  7.2 164.1 %all-gather.3.cloned.1.call-start = ((), (), s32[]{:S(2)}) async-start(), calls=%async_computation.2 | async-start | bytes 17301504 | tf_op jit(solution)/shard_map/all_gather | solution.py:104
  22.0 187.1 %all-gather.5.cloned.1.call-start = ((), (), s32[]{:S(2)}) async-start(), calls=%async_computation.4 | async-start | bytes 2359296 | tf_op jit(solution)/shard_map/all_gather | solution.py:112
  23.9 90.7 %collective-permute-start.9 = (bf16[128,128]{0,1:T(8,128)(2,1)S(1)}, bf16[128,128]{0,1:T(8,128)(2,1)S(1)}, u32[]{:S(2)}, u32[]{:S(2)}) collective-permute-start(bf16[128,128]{0,1:T(8,128)(2,1)S(1)} %pad_maximum_fusion.2), channel_id=1, source_target_pairs={{0,72},{8,80},{16,88},{24,96},{32,104},{40,112},{48,120},{56,128},... | collective-permute-start | bytes 98312 | tf_op jit(solution)/shard_map/ppermute | solution.py:19
  33.6 83.0 %collective-permute-start.10 = (bf16[128,128]{0,1:T(8,128)(2,1)S(1)}, bf16[128,128]{0,1:T(8,128)(2,1)S(1)}, u32[]{:S(2)}, u32[]{:S(2)}) collective-permute-start(bf16[128,128]{0,1:T(8,128)(2,1)S(1)} %pad_maximum_fusion.2), channel_id=1, source_target_pairs={{0,64},{8,72},{16,80},{24,88},{32,96},{40,104},{48,112},{56,120},{... | collective-permute-start | bytes 98312 | tf_op jit(solution)/shard_map/ppermute | solution.py:19
  36.7 86.3 %collective-permute-start.11 = (bf16[128,128]{0,1:T(8,128)(2,1)S(1)}, bf16[128,128]{0,1:T(8,128)(2,1)S(1)}, u32[]{:S(2)}, u32[]{:S(2)}) collective-permute-start(bf16[128,128]{0,1:T(8,128)(2,1)S(1)} %pad_maximum_fusion.2), channel_id=1, source_target_pairs={{0,56},{8,64},{16,72},{24,80},{32,88},{40,96},{48,104},{56,112},{6... | collective-permute-start | bytes 98312 | tf_op jit(solution)/shard_map/ppermute | solution.py:19
  38.6 86.4 %collective-permute-start.12 = (bf16[128,128]{0,1:T(8,128)(2,1)S(1)}, bf16[128,128]{0,1:T(8,128)(2,1)S(1)}, u32[]{:S(2)}, u32[]{:S(2)}) collective-permute-start(bf16[128,128]{0,1:T(8,128)(2,1)S(1)} %pad_maximum_fusion.2), channel_id=1, source_target_pairs={{0,48},{8,56},{16,64},{24,72},{32,80},{40,88},{48,96},{56,104},{64... | collective-permute-start | bytes 98312 | tf_op jit(solution)/shard_map/ppermute | solution.py:19
  40.8 7.7 %collective-permute-start = (s32[128]{0:T(128)}, s32[128]{0:T(128)S(1)}, u32[]{:S(2)}, u32[]{:S(2)}) collective-permute-start(s32[128]{0:T(128)} %param.13), channel_id=1, source_target_pairs={{0,72},{8,80},{16,88},{24,96},{32,104},{40,112},{48,120},{56,128},... | collective-permute-start | bytes 1544 | tf_op jit(solution)/shard_map/ppermute | solution.py:19
  42.8 277.2 %reduce-scatter.2.cloned.1.call-start = ((), (), s32[]{:S(2)}) async-start(), calls=%async_computation.3 | async-start | bytes 2359296 | tf_op jit(solution)/shard_map/reduce_scatter | solution.py:152
  48.5 5.5 %collective-permute-start.1 = (s32[128]{0:T(128)}, s32[128]{0:T(128)S(1)}, u32[]{:S(2)}, u32[]{:S(2)}) collective-permute-start(s32[128]{0:T(128)} %param.13), channel_id=1, source_target_pairs={{0,64},{8,72},{16,80},{24,88},{32,96},{40,104},{48,112},{56,120},{... | collective-permute-start | bytes 1544 | tf_op jit(solution)/shard_map/ppermute | solution.py:19
  54.0 8.3 %collective-permute-start.2 = (s32[128]{0:T(128)}, s32[128]{0:T(128)S(1)}, u32[]{:S(2)}, u32[]{:S(2)}) collective-permute-start(s32[128]{0:T(128)} %param.13), channel_id=1, source_target_pairs={{0,56},{8,64},{16,72},{24,80},{32,88},{40,96},{48,104},{56,112},{6... | collective-permute-start | bytes 1544 | tf_op jit(solution)/shard_map/ppermute | solution.py:19
  62.3 7.7 %collective-permute-start.3 = (s32[128]{0:T(128)}, s32[128]{0:T(128)S(1)}, u32[]{:S(2)}, u32[]{:S(2)}) collective-permute-start(s32[128]{0:T(128)} %param.13), channel_id=1, source_target_pairs={{0,48},{8,56},{16,64},{24,72},{32,80},{40,88},{48,96},{56,104},{64... | collective-permute-start | bytes 1544 | tf_op jit(solution)/shard_map/ppermute | solution.py:19
  70.1 7.6 %collective-permute-start.4 = (s32[128]{0:T(128)}, s32[128]{0:T(128)S(1)}, u32[]{:S(2)}, u32[]{:S(2)}) collective-permute-start(s32[128]{0:T(128)} %param.13), channel_id=1, source_target_pairs={{0,40},{8,48},{16,56},{24,64},{32,72},{40,80},{48,88},{56,96},{64,... | collective-permute-start | bytes 1544 | tf_op jit(solution)/shard_map/ppermute | solution.py:19
  77.6 6.5 %collective-permute-start.5 = (s32[128]{0:T(128)}, s32[128]{0:T(128)S(1)}, u32[]{:S(2)}, u32[]{:S(2)}) collective-permute-start(s32[128]{0:T(128)} %param.13), channel_id=1, source_target_pairs={{0,32},{8,40},{16,48},{24,56},{32,64},{40,72},{48,80},{56,88},{64,... | collective-permute-start | bytes 1544 | tf_op jit(solution)/shard_map/ppermute | solution.py:19
  84.1 11.1 %collective-permute-start.6 = (s32[128]{0:T(128)}, s32[128]{0:T(128)S(1)}, u32[]{:S(2)}, u32[]{:S(2)}) collective-permute-start(s32[128]{0:T(128)} %param.13), channel_id=1, source_target_pairs={{0,24},{8,32},{16,40},{24,48},{32,56},{40,64},{48,72},{56,80},{64,... | collective-permute-start | bytes 1544 | tf_op jit(solution)/shard_map/ppermute | solution.py:19
  95.2 6.9 %collective-permute-start.7 = (s32[128]{0:T(128)}, s32[128]{0:T(128)S(1)}, u32[]{:S(2)}, u32[]{:S(2)}) collective-permute-start(s32[128]{0:T(128)} %param.13), channel_id=1, source_target_pairs={{0,16},{8,24},{16,32},{24,40},{32,48},{40,56},{48,64},{56,72},{64,... | collective-permute-start | bytes 1544 | tf_op jit(solution)/shard_map/ppermute | solution.py:19
  102.1 5.6 %collective-permute-start.8 = (s32[128]{0:T(128)}, s32[128]{0:T(128)S(1)}, u32[]{:S(2)}, u32[]{:S(2)}) collective-permute-start(s32[128]{0:T(128)} %param.13), channel_id=1, source_target_pairs={{0,8},{8,16},{16,24},{24,32},{32,40},{40,48},{48,56},{56,64},{64,7... | collective-permute-start | bytes 1544 | tf_op jit(solution)/shard_map/ppermute | solution.py:19
  107.7 22.2 %collective-permute-start.13 = (bf16[128,128]{0,1:T(8,128)(2,1)S(1)}, bf16[128,128]{0,1:T(8,128)(2,1)S(1)}, u32[]{:S(2)}, u32[]{:S(2)}) collective-permute-start(bf16[128,128]{0,1:T(8,128)(2,1)S(1)} %pad_maximum_fusion.2), channel_id=1, source_target_pairs={{0,40},{8,48},{16,56},{24,64},{32,72},{40,80},{48,88},{56,96},{64,... | collective-permute-start | bytes 98312 | tf_op jit(solution)/shard_map/ppermute | solution.py:19
  114.6 17.2 %collective-permute-start.14 = (bf16[128,128]{0,1:T(8,128)(2,1)S(1)}, bf16[128,128]{0,1:T(8,128)(2,1)S(1)}, u32[]{:S(2)}, u32[]{:S(2)}) collective-permute-start(bf16[128,128]{0,1:T(8,128)(2,1)S(1)} %pad_maximum_fusion.2), channel_id=1, source_target_pairs={{0,32},{8,40},{16,48},{24,56},{32,64},{40,72},{48,80},{56,88},{64,... | collective-permute-start | bytes 98312 | tf_op jit(solution)/shard_map/ppermute | solution.py:19
  116.6 17.2 %collective-permute-start.15 = (bf16[128,128]{0,1:T(8,128)(2,1)S(1)}, bf16[128,128]{0,1:T(8,128)(2,1)S(1)}, u32[]{:S(2)}, u32[]{:S(2)}) collective-permute-start(bf16[128,128]{0,1:T(8,128)(2,1)S(1)} %pad_maximum_fusion.2), channel_id=1, source_target_pairs={{0,24},{8,32},{16,40},{24,48},{32,56},{40,64},{48,72},{56,80},{64,... | collective-permute-start | bytes 98312 | tf_op jit(solution)/shard_map/ppermute | solution.py:19
  123.1 12.7 %collective-permute-start.16 = (bf16[128,128]{0,1:T(8,128)(2,1)S(1)}, bf16[128,128]{0,1:T(8,128)(2,1)S(1)}, u32[]{:S(2)}, u32[]{:S(2)}) collective-permute-start(bf16[128,128]{0,1:T(8,128)(2,1)S(1)} %pad_maximum_fusion.2), channel_id=1, source_target_pairs={{0,16},{8,24},{16,32},{24,40},{32,48},{40,56},{48,64},{56,72},{64,... | collective-permute-start | bytes 98312 | tf_op jit(solution)/shard_map/ppermute | solution.py:19
  125.0 12.7 %collective-permute-start.17 = (bf16[128,128]{0,1:T(8,128)(2,1)S(1)}, bf16[128,128]{0,1:T(8,128)(2,1)S(1)}, u32[]{:S(2)}, u32[]{:S(2)}) collective-permute-start(bf16[128,128]{0,1:T(8,128)(2,1)S(1)} %pad_maximum_fusion.2), channel_id=1, source_target_pairs={{0,8},{8,16},{16,24},{24,32},{32,40},{40,48},{48,56},{56,64},{64,7... | collective-permute-start | bytes 98312 | tf_op jit(solution)/shard_map/ppermute | solution.py:19
  129.9 19.2 %collective-permute-start.18 = (bf16[128,128]{1,0:T(8,128)(2,1)}, bf16[128,128]{1,0:T(8,128)(2,1)S(1)}, u32[]{:S(2)}, u32[]{:S(2)}) collective-permute-start(bf16[128,128]{1,0:T(8,128)(2,1)} %param.10), channel_id=1, source_target_pairs={{0,72},{8,80},{16,88},{24,96},{32,104},{40,112},{48,120},{56,128},... | collective-permute-start | bytes 98312 | tf_op jit(solution)/shard_map/ppermute | solution.py:19
  131.9 19.2 %collective-permute-start.19 = (bf16[128,128]{1,0:T(8,128)(2,1)}, bf16[128,128]{1,0:T(8,128)(2,1)S(1)}, u32[]{:S(2)}, u32[]{:S(2)}) collective-permute-start(bf16[128,128]{1,0:T(8,128)(2,1)} %param.10), channel_id=1, source_target_pairs={{0,64},{8,72},{16,80},{24,88},{32,96},{40,104},{48,112},{56,120},{... | collective-permute-start | bytes 98312 | tf_op jit(solution)/shard_map/ppermute | solution.py:19
  133.8 19.2 %collective-permute-start.20 = (bf16[128,128]{1,0:T(8,128)(2,1)}, bf16[128,128]{1,0:T(8,128)(2,1)S(1)}, u32[]{:S(2)}, u32[]{:S(2)}) collective-permute-start(bf16[128,128]{1,0:T(8,128)(2,1)} %param.10), channel_id=1, source_target_pairs={{0,56},{8,64},{16,72},{24,80},{32,88},{40,96},{48,104},{56,112},{6... | collective-permute-start | bytes 98312 | tf_op jit(solution)/shard_map/ppermute | solution.py:19
  135.8 19.2 %collective-permute-start.21 = (bf16[128,128]{1,0:T(8,128)(2,1)}, bf16[128,128]{1,0:T(8,128)(2,1)S(1)}, u32[]{:S(2)}, u32[]{:S(2)}) collective-permute-start(bf16[128,128]{1,0:T(8,128)(2,1)} %param.10), channel_id=1, source_target_pairs={{0,48},{8,56},{16,64},{24,72},{32,80},{40,88},{48,96},{56,104},{64... | collective-permute-start | bytes 98312 | tf_op jit(solution)/shard_map/ppermute | solution.py:19
  137.8 19.4 %collective-permute-start.22 = (bf16[128,128]{1,0:T(8,128)(2,1)}, bf16[128,128]{1,0:T(8,128)(2,1)S(1)}, u32[]{:S(2)}, u32[]{:S(2)}) collective-permute-start(bf16[128,128]{1,0:T(8,128)(2,1)} %param.10), channel_id=1, source_target_pairs={{0,40},{8,48},{16,56},{24,64},{32,72},{40,80},{48,88},{56,96},{64,... | collective-permute-start | bytes 98312 | tf_op jit(solution)/shard_map/ppermute | solution.py:19
  149.2 8.1 %collective-permute-start.23 = (bf16[128,128]{1,0:T(8,128)(2,1)S(1)}, bf16[128,128]{1,0:T(8,128)(2,1)S(1)}, u32[]{:S(2)}, u32[]{:S(2)}) collective-permute-start(bf16[128,128]{1,0:T(8,128)(2,1)S(1)} %copy-done.10), channel_id=1, source_target_pairs={{0,32},{8,40},{16,48},{24,56},{32,64},{40,72},{48,80},{56,88},{64,... | collective-permute-start | bytes 98312 | tf_op jit(solution)/shard_map/ppermute | solution.py:19
  151.1 8.5 %collective-permute-start.24 = (bf16[128,128]{1,0:T(8,128)(2,1)S(1)}, bf16[128,128]{1,0:T(8,128)(2,1)S(1)}, u32[]{:S(2)}, u32[]{:S(2)}) collective-permute-start(bf16[128,128]{1,0:T(8,128)(2,1)S(1)} %copy-done.10), channel_id=1, source_target_pairs={{0,24},{8,32},{16,40},{24,48},{32,56},{40,64},{48,72},{56,80},{64,... | collective-permute-start | bytes 98312 | tf_op jit(solution)/shard_map/ppermute | solution.py:19
  153.1 8.4 %collective-permute-start.25 = (bf16[128,128]{1,0:T(8,128)(2,1)S(1)}, bf16[128,128]{1,0:T(8,128)(2,1)S(1)}, u32[]{:S(2)}, u32[]{:S(2)}) collective-permute-start(bf16[128,128]{1,0:T(8,128)(2,1)S(1)} %copy-done.10), channel_id=1, source_target_pairs={{0,16},{8,24},{16,32},{24,40},{32,48},{40,56},{48,64},{56,72},{64,... | collective-permute-start | bytes 98312 | tf_op jit(solution)/shard_map/ppermute | solution.py:19
  155.0 6.4 %collective-permute-start.26 = (bf16[128,128]{1,0:T(8,128)(2,1)S(1)}, bf16[128,128]{1,0:T(8,128)(2,1)S(1)}, u32[]{:S(2)}, u32[]{:S(2)}) collective-permute-start(bf16[128,128]{1,0:T(8,128)(2,1)S(1)} %copy-done.10), channel_id=1, source_target_pairs={{0,8},{8,16},{16,24},{24,32},{32,40},{40,48},{48,56},{56,64},{64,7... | collective-permute-start | bytes 98312 | tf_op jit(solution)/shard_map/ppermute | solution.py:19
  254.0 23.6 %collective-permute-start.27 = (bf16[128,128]{0,1:T(8,128)(2,1)S(1)}, bf16[128,128]{0,1:T(8,128)(2,1)S(1)}, u32[]{:S(2)}, u32[]{:S(2)}) collective-permute-start(bf16[128,128]{0,1:T(8,128)(2,1)S(1)} %get-tuple-element.41), channel_id=1, source_target_pairs={{8,0},{16,8},{24,16},{32,24},{40,32},{48,40},{56,48},{64,56},{72,6... | collective-permute-start | bytes 98312 | tf_op jit(solution)/shard_map/ppermute | solution.py:19
  261.9 19.7 %collective-permute-start.28 = (bf16[128,128]{0,1:T(8,128)(2,1)S(1)}, bf16[128,128]{0,1:T(8,128)(2,1)S(1)}, u32[]{:S(2)}, u32[]{:S(2)}) collective-permute-start(bf16[128,128]{0,1:T(8,128)(2,1)S(1)} %get-tuple-element.49), channel_id=1, source_target_pairs={{16,0},{24,8},{32,16},{40,24},{48,32},{56,40},{64,48},{72,56},{80,... | collective-permute-start | bytes 98312 | tf_op jit(solution)/shard_map/ppermute | solution.py:19
  266.2 17.4 %collective-permute-start.29 = (bf16[128,128]{0,1:T(8,128)(2,1)S(1)}, bf16[128,128]{0,1:T(8,128)(2,1)S(1)}, u32[]{:S(2)}, u32[]{:S(2)}) collective-permute-start(bf16[128,128]{0,1:T(8,128)(2,1)S(1)} %get-tuple-element.48), channel_id=1, source_target_pairs={{24,0},{32,8},{40,16},{48,24},{56,32},{64,40},{72,48},{80,56},{88,... | collective-permute-start | bytes 98312 | tf_op jit(solution)/shard_map/ppermute | solution.py:19
  268.8 16.7 %collective-permute-start.30 = (bf16[128,128]{0,1:T(8,128)(2,1)S(1)}, bf16[128,128]{0,1:T(8,128)(2,1)S(1)}, u32[]{:S(2)}, u32[]{:S(2)}) collective-permute-start(bf16[128,128]{0,1:T(8,128)(2,1)S(1)} %get-tuple-element.47), channel_id=1, source_target_pairs={{32,0},{40,8},{48,16},{56,24},{64,32},{72,40},{80,48},{88,56},{96,... | collective-permute-start | bytes 98312 | tf_op jit(solution)/shard_map/ppermute | solution.py:19
  270.9 17.4 %collective-permute-start.31 = (bf16[128,128]{0,1:T(8,128)(2,1)}, bf16[128,128]{0,1:T(8,128)(2,1)}, u32[]{:S(2)}, u32[]{:S(2)}) collective-permute-start(bf16[128,128]{0,1:T(8,128)(2,1)} %get-tuple-element.46), channel_id=1, source_target_pairs={{40,0},{48,8},{56,16},{64,24},{72,32},{80,40},{88,48},{96,56},{104... | collective-permute-start | bytes 98312 | tf_op jit(solution)/shard_map/ppermute | solution.py:19
  277.6 13.0 %collective-permute-start.32 = (bf16[128,128]{0,1:T(8,128)(2,1)}, bf16[128,128]{0,1:T(8,128)(2,1)S(1)}, u32[]{:S(2)}, u32[]{:S(2)}) collective-permute-start(bf16[128,128]{0,1:T(8,128)(2,1)} %get-tuple-element.45), channel_id=1, source_target_pairs={{48,0},{56,8},{64,16},{72,24},{80,32},{88,40},{96,48},{104,56},{11... | collective-permute-start | bytes 98312 | tf_op jit(solution)/shard_map/ppermute | solution.py:19
  281.6 11.0 %collective-permute-start.33 = (bf16[128,128]{0,1:T(8,128)(2,1)}, bf16[128,128]{0,1:T(8,128)(2,1)S(1)}, u32[]{:S(2)}, u32[]{:S(2)}) collective-permute-start(bf16[128,128]{0,1:T(8,128)(2,1)} %get-tuple-element.44), channel_id=1, source_target_pairs={{56,0},{64,8},{72,16},{80,24},{88,32},{96,40},{104,48},{112,56},{1... | collective-permute-start | bytes 98312 | tf_op jit(solution)/shard_map/ppermute | solution.py:19
  283.6 12.8 %collective-permute-start.34 = (bf16[128,128]{0,1:T(8,128)(2,1)}, bf16[128,128]{0,1:T(8,128)(2,1)S(1)}, u32[]{:S(2)}, u32[]{:S(2)}) collective-permute-start(bf16[128,128]{0,1:T(8,128)(2,1)} %get-tuple-element.43), channel_id=1, source_target_pairs={{64,0},{72,8},{80,16},{88,24},{96,32},{104,40},{112,48},{120,56},{... | collective-permute-start | bytes 98312 | tf_op jit(solution)/shard_map/ppermute | solution.py:19
  285.5 12.8 %collective-permute-start.35 = (bf16[128,128]{0,1:T(8,128)(2,1)}, bf16[128,128]{0,1:T(8,128)(2,1)S(1)}, u32[]{:S(2)}, u32[]{:S(2)}) collective-permute-start(bf16[128,128]{0,1:T(8,128)(2,1)} %get-tuple-element.42), channel_id=1, source_target_pairs={{72,0},{80,8},{88,16},{96,24},{104,32},{112,40},{120,48},{128,56},... | collective-permute-start | bytes 98312 | tf_op jit(solution)/shard_map/ppermute | solution.py:19
  288.4 13.7 %collective-permute-start.36 = (bf16[128,128]{1,0:T(8,128)(2,1)}, bf16[128,128]{1,0:T(8,128)(2,1)S(1)}, u32[]{:S(2)}, u32[]{:S(2)}) collective-permute-start(bf16[128,128]{1,0:T(8,128)(2,1)} %get-tuple-element.32), channel_id=1, source_target_pairs={{8,0},{16,8},{24,16},{32,24},{40,32},{48,40},{56,48},{64,56},{72,6... | collective-permute-start | bytes 98312 | tf_op jit(solution)/shard_map/ppermute | solution.py:19
  290.7 13.4 %collective-permute-start.37 = (bf16[128,128]{1,0:T(8,128)(2,1)}, bf16[128,128]{1,0:T(8,128)(2,1)S(1)}, u32[]{:S(2)}, u32[]{:S(2)}) collective-permute-start(bf16[128,128]{1,0:T(8,128)(2,1)} %get-tuple-element.40), channel_id=1, source_target_pairs={{16,0},{24,8},{32,16},{40,24},{48,32},{56,40},{64,48},{72,56},{80,... | collective-permute-start | bytes 98312 | tf_op jit(solution)/shard_map/ppermute | solution.py:19
  292.6 13.4 %collective-permute-start.38 = (bf16[128,128]{1,0:T(8,128)(2,1)}, bf16[128,128]{1,0:T(8,128)(2,1)S(1)}, u32[]{:S(2)}, u32[]{:S(2)}) collective-permute-start(bf16[128,128]{1,0:T(8,128)(2,1)} %get-tuple-element.39), channel_id=1, source_target_pairs={{24,0},{32,8},{40,16},{48,24},{56,32},{64,40},{72,48},{80,56},{88,... | collective-permute-start | bytes 98312 | tf_op jit(solution)/shard_map/ppermute | solution.py:19
  296.4 11.5 %collective-permute-start.39 = (bf16[128,128]{1,0:T(8,128)(2,1)}, bf16[128,128]{1,0:T(8,128)(2,1)S(1)}, u32[]{:S(2)}, u32[]{:S(2)}) collective-permute-start(bf16[128,128]{1,0:T(8,128)(2,1)} %get-tuple-element.38), channel_id=1, source_target_pairs={{32,0},{40,8},{48,16},{56,24},{64,32},{72,40},{80,48},{88,56},{96,... | collective-permute-start | bytes 98312 | tf_op jit(solution)/shard_map/ppermute | solution.py:19
  298.4 12.2 %collective-permute-start.40 = (bf16[128,128]{1,0:T(8,128)(2,1)}, bf16[128,128]{1,0:T(8,128)(2,1)S(1)}, u32[]{:S(2)}, u32[]{:S(2)}) collective-permute-start(bf16[128,128]{1,0:T(8,128)(2,1)} %get-tuple-element.37), channel_id=1, source_target_pairs={{40,0},{48,8},{56,16},{64,24},{72,32},{80,40},{88,48},{96,56},{104... | collective-permute-start | bytes 98312 | tf_op jit(solution)/shard_map/ppermute | solution.py:19
  302.1 9.7 %collective-permute-start.41 = (bf16[128,128]{1,0:T(8,128)(2,1)}, bf16[128,128]{1,0:T(8,128)(2,1)S(1)}, u32[]{:S(2)}, u32[]{:S(2)}) collective-permute-start(bf16[128,128]{1,0:T(8,128)(2,1)} %get-tuple-element.36), channel_id=1, source_target_pairs={{48,0},{56,8},{64,16},{72,24},{80,32},{88,40},{96,48},{104,56},{11... | collective-permute-start | bytes 98312 | tf_op jit(solution)/shard_map/ppermute | solution.py:19
  304.1 9.5 %collective-permute-start.42 = (bf16[128,128]{1,0:T(8,128)(2,1)}, bf16[128,128]{1,0:T(8,128)(2,1)S(1)}, u32[]{:S(2)}, u32[]{:S(2)}) collective-permute-start(bf16[128,128]{1,0:T(8,128)(2,1)} %get-tuple-element.35), channel_id=1, source_target_pairs={{56,0},{64,8},{72,16},{80,24},{88,32},{96,40},{104,48},{112,56},{1... | collective-permute-start | bytes 98312 | tf_op jit(solution)/shard_map/ppermute | solution.py:19
  306.0 9.5 %collective-permute-start.43 = (bf16[128,128]{1,0:T(8,128)(2,1)S(1)}, bf16[128,128]{1,0:T(8,128)(2,1)S(1)}, u32[]{:S(2)}, u32[]{:S(2)}) collective-permute-start(bf16[128,128]{1,0:T(8,128)(2,1)S(1)} %get-tuple-element.34), channel_id=1, source_target_pairs={{64,0},{72,8},{80,16},{88,24},{96,32},{104,40},{112,48},{120,56},{... | collective-permute-start | bytes 98312 | tf_op jit(solution)/shard_map/ppermute | solution.py:19
  307.9 11.3 %collective-permute-start.44 = (bf16[128,128]{1,0:T(8,128)(2,1)S(1)}, bf16[128,128]{1,0:T(8,128)(2,1)S(1)}, u32[]{:S(2)}, u32[]{:S(2)}) collective-permute-start(bf16[128,128]{1,0:T(8,128)(2,1)S(1)} %get-tuple-element.33), channel_id=1, source_target_pairs={{72,0},{80,8},{88,16},{96,24},{104,32},{112,40},{120,48},{128,56},... | collective-permute-start | bytes 98312 | tf_op jit(solution)/shard_map/ppermute | solution.py:19
  (19 other events, 724.0 us)
Sparse Core Ops, SparseCore 0:
  22.1 144.2 all-gather.2
  168.2 40.7 all-gather.4
  244.9 47.1 reduce-scatter.1
where the time goes:
time: 329 us; the launch traced here: 326 us
  starting transfers between devices  149 us (45%)
  matrix products  62.5 us (19%)
  waiting for transfers between devices  55.1 us (17%)
  local copies, waits for them, and re-layouts  21.4 us (7%)
  between operations  15.1 us (5%)
  blocking collectives  13.7 us (4%)
  other arithmetic  9.84 us (3%)
    ppermute x45, starting transfers between devices, shifted(): return lax.ppermute(block, axis, route)  149 us
    ppermute x45, waiting for transfers between devices, shifted(): return lax.ppermute(block, axis, route)  31.6 us
    all_gather x1, waiting for transfers between devices, per_device(): lax.all_gather(out_grad, 'kv', axis=1, tiled=True)  23.4 us
    transpose x1, local copies, waits for them, and re-layouts, per_device(): row_weight = stripes.reshape(row_count, seq_count, kv_count, -1).transpos...  14.3 us
    all_to_all x1, blocking collectives, per_device(): lax.all_to_all(out_weight, 'kv', split_axis=0, concat_axis=1, tiled=True)  13.7 us
    dot_general x1, matrix products, per_device(): out_terms = jnp.dot(attn, row_weight, preferred_element_type=jnp.float32)  13.1 us
    dot_general x1, matrix products, per_device(): lax.dot_general(lax.all_gather(out_grad, 'kv', axis=1, tiled=True), row_w...  13 us
    dot_general x8, matrix products, attend(): lax.dot_general(dscore, query, columns, preferred_element_type=jnp.float32)  10.3 us
  transfers between devices with their start and end apart: 48, of which 16 were waited for; matrix products, arithmetic and copies ran while one was open for 17% of the time, Pallas kernels for 0%

commit v1 on v0

--- a/solution.py
+++ b/solution.py
@@ -3,20 +3,31 @@
 import jax
 import jax.numpy as jnp
 from jax import lax
+from jax.sharding import Mesh
 from jax.sharding import PartitionSpec as P
 
 HD = 128
 BLK = 128
 REACH = 9
 
+SEQ = ("sz", "core")
 
 rope_base = 1000000.0
 
 
-def shifted(block, axis, distance):
-    devices = range(lax.axis_size(axis))
+def seq_size():
+    return lax.axis_size("sz") * lax.axis_size("core")
+
+
+def seq_index():
+    return lax.axis_index("sz") * lax.axis_size("core") + lax.axis_index("core")
+
+
+def shifted(block, distance):
+    count = seq_size()
+    devices = range(count)
     route = [(i - distance, i) for i in devices if i - distance in devices]
-    return lax.ppermute(block, axis, route)
+    return lax.ppermute(block, SEQ, route)
 
 
 def rope_tables(positions):
@@ -80,15 +91,30 @@
     return (output, dquery, dkey, dvalue)
 
 
+def gather_window(packed):
+    one = jnp.concatenate([shifted(packed, 1), packed], axis=0)
+    two = jnp.concatenate([shifted(one, 2), one], axis=0)
+    four = jnp.concatenate([shifted(two, 4), two], axis=0)
+    far = shifted(one, 8)
+    return jnp.concatenate([far, four], axis=0)
+
+
+def return_window(pieces):
+    far = shifted(pieces[:2].astype(jnp.bfloat16), -8).astype(jnp.float32)
+    four = pieces[2:]
+    two = four[4:] + shifted(four[:4].astype(jnp.bfloat16), -4).astype(jnp.float32)
+    one = two[2:] + shifted(two[:2].astype(jnp.bfloat16), -2).astype(jnp.float32) + far
+    return one[1] + shifted(one[:1].astype(jnp.bfloat16), -1).astype(jnp.float32)[0]
+
+
 def per_device(queries, keys, values, out_weight, out_grad, doc_ids, block_mask, positions):
     length = queries.shape[0]
     groups = keys.shape[1] // HD
     heads = queries.shape[1] // HD
     per_group = heads // groups
-    kv_count = lax.axis_size("kv")
-    seq_count = lax.axis_size("seq")
-    shard = lax.axis_index("seq")
-    contract = (((1,), (1,)), ((), ()))
+    n_sz = lax.axis_size("sz")
+    n_core = lax.axis_size("core")
+    shard = seq_index()
     cosine, sine = rope_tables(positions)
     q_rot = (
         rotate(queries.astype(jnp.float32).reshape(length, heads, HD), cosine, sine, 1.0)
@@ -100,31 +126,30 @@
         .astype(jnp.bfloat16)
         .reshape(length, groups * HD)
     )
-    pieces = lax.all_to_all(out_weight, "kv", split_axis=0, concat_axis=1, tiled=True)
-    stripes = lax.all_gather(pieces, "seq", axis=1, tiled=True)
-    row_count = stripes.shape[0]
-    row_weight = (
-        stripes.reshape(row_count, seq_count, kv_count, -1)
+    col_w = out_weight.shape[1]
+    w_cols = lax.all_gather(out_weight, "sz", axis=1, tiled=True)
+    w_cols = lax.all_gather(w_cols, "core", axis=1, tiled=True)
+    og_perm = (
+        out_grad.reshape(length, n_sz, n_core, col_w)
         .transpose(0, 2, 1, 3)
-        .reshape(row_count, -1)
-    )
-    head_grad = lax.dot_general(
-        lax.all_gather(out_grad, "kv", axis=1, tiled=True),
-        row_weight,
-        contract,
-        preferred_element_type=jnp.float32,
-    ).astype(jnp.bfloat16)
-    key_parts = []
-    value_parts = []
-    doc_parts = []
-    for reach in range(REACH, 0, -1):
-        moved = shifted((k_rot, values, doc_ids), "seq", reach)
-        key_parts.append(moved[0])
-        value_parts.append(moved[1])
-        doc_parts.append(moved[2])
-    key_win = jnp.concatenate(key_parts + [k_rot], axis=0)
-    value_win = jnp.concatenate(value_parts + [values], axis=0)
-    doc_win = jnp.concatenate(doc_parts + [doc_ids], axis=0)
+        .reshape(length, n_sz * n_core * col_w)
+    )
+    contract = (((1,), (1,)), ((), ()))
+    hg_part = lax.dot_general(og_perm, w_cols, contract, preferred_element_type=jnp.float32)
+    head_grad = lax.psum_scatter(
+        hg_part.astype(jnp.bfloat16), "kv", scatter_dimension=1, tiled=True
+    )
+    width = keys.shape[1]
+    doc_row = jnp.zeros((1, 2 * width), jnp.bfloat16).at[0, :length].set(
+        doc_ids.astype(jnp.bfloat16)
+    )
+    packed = jnp.concatenate(
+        [jnp.concatenate([k_rot, values], axis=1), doc_row], axis=0
+    )[None]
+    win = gather_window(packed)
+    key_win = win[:, :length, :width].reshape(-1, width)
+    value_win = win[:, :length, width:].reshape(-1, width)
+    doc_win = win[:, length, :length].reshape(-1).astype(jnp.int32)
     blocks_dev = length // BLK
     mask_pad = jnp.pad(block_mask, ((0, 0), (REACH * blocks_dev, 0)))
     mask_rows = lax.dynamic_slice_in_dim(mask_pad, shard * blocks_dev, (REACH + 1) * blocks_dev, 1)
@@ -148,25 +173,26 @@
         dvalue_sum = dvalue_sum + dvalue
     attn = jnp.concatenate(outputs, axis=1)
     dq_rot = jnp.stack(dqueries, axis=1)
-    out_terms = jnp.dot(attn, row_weight, preferred_element_type=jnp.float32)
-    layer_out = lax.psum_scatter(
-        out_terms.astype(jnp.bfloat16), "kv", scatter_dimension=1, tiled=True
-    )
-    own = REACH * length
-    dk_total = dkey_sum[own:]
-    dv_total = dvalue_sum[own:]
-    for reach in range(1, REACH + 1):
-        slot = (REACH - reach) * length
-        back = (
-            shifted(dkey_sum[slot : slot + length].astype(jnp.bfloat16), "seq", -reach).astype(
-                jnp.float32
-            ),
-            shifted(dvalue_sum[slot : slot + length].astype(jnp.bfloat16), "seq", -reach).astype(
-                jnp.float32
-            ),
-        )
-        dk_total = dk_total + back[0]
-        dv_total = dv_total + back[1]
+    attn_all = lax.all_gather(attn, "kv", axis=1, tiled=True)
+    kv_count = lax.axis_size("kv")
+    rows = attn.shape[1]
+    parts = jnp.einsum(
+        "tgr,grc->gtc",
+        attn_all.reshape(length, kv_count, rows),
+        w_cols.reshape(kv_count, rows, -1),
+        preferred_element_type=jnp.float32,
+    ).astype(jnp.bfloat16)
+    parts = lax.optimization_barrier(parts)
+    out_perm = jnp.sum(parts.astype(jnp.float32), axis=0).astype(jnp.bfloat16)
+    layer_out = (
+        out_perm.reshape(length, n_core, n_sz, col_w)
+        .transpose(0, 2, 1, 3)
+        .reshape(length, n_sz * n_core * col_w)
+    )
+    dkv = jnp.concatenate([dkey_sum, dvalue_sum], axis=1).reshape(REACH + 1, length, 2 * HD)
+    dkv_total = return_window(dkv)
+    dk_total = dkv_total[:, :HD]
+    dv_total = dkv_total[:, HD:]
     query_grad = rotate(dq_rot, cosine, sine, -1.0).astype(jnp.bfloat16).reshape(length, heads * HD)
     key_grad = (
         rotate(dk_total.reshape(length, groups, HD), cosine, sine, -1.0)
@@ -178,17 +204,20 @@
 
 
 def solution(mesh):
+    n_seq, n_kv = mesh.devices.shape
+    cores = 2 if n_seq % 2 == 0 else 1
+    grid = Mesh(mesh.devices.reshape(n_seq // cores, cores, n_kv), ("sz", "core", "kv"))
     in_specs = (
-        P("seq", "kv"),
-        P("seq", "kv"),
-        P("seq", "kv"),
-        P(None, ("kv", "seq")),
-        P("seq", "kv"),
-        P("seq"),
-        P("seq", None),
-        P(None, "seq"),
-    )
-    out_specs = (P("seq", "kv"), P("seq", "kv"), P("seq", "kv"), P("seq", "kv"))
+        P(SEQ, "kv"),
+        P(SEQ, "kv"),
+        P(SEQ, "kv"),
+        P(None, ("kv",) + SEQ),
+        P(SEQ, "kv"),
+        P(SEQ),
+        P(SEQ, None),
+        P(None, SEQ),
+    )
+    out_specs = (P(SEQ, "kv"), P(SEQ, "kv"), P(SEQ, "kv"), P(SEQ, "kv"))
     return jax.shard_map(
-        per_device, mesh=mesh, in_specs=in_specs, out_specs=out_specs, check_vma=False
-    )
+        per_device, mesh=grid, in_specs=in_specs, out_specs=out_specs, check_vma=False
+    )

time: 329 us -> 342 us (1.040)
  waiting for transfers between devices: 55.1 us -> 197 us
  starting transfers between devices: 149 us -> 33.2 us
  blocking collectives: 13.7 us -> 0 us
  matrix products: 62.5 us -> 52.4 us
  local copies, waits for them, and re-layouts: 21.4 us -> 30.9 us
    all_gather x2 -> x3, waiting for transfers between devices: 23.4 us -> 147 us  [the longest x1 138 us: per_device(): w_cols = lax.all_gather(out_weight, 'sz', axis=1, tiled=True)]
    ppermute x45 -> x8, starting transfers between devices: 149 us -> 32.8 us  [shifted(): return lax.ppermute(block, SEQ, route)]
    reduce_scatter x1, waiting for transfers between devices: 0.01 us -> 35.4 us  [per_device(): lax.psum_scatter(hg_part.astype(jnp.bfloat16), 'kv', scatter_dimension=1,...]
    all_gather x0 -> x1, local copies, waits for them, and re-layouts: none -> 22.5 us  [per_device(): w_cols = lax.all_gather(w_cols, 'core', axis=1, tiled=True)]
    ppermute x45 -> x8, waiting for transfers between devices: 31.6 us -> 14.2 us  [shifted(): return lax.ppermute(block, SEQ, route)]
    transpose x1 -> x2, local copies, waits for them, and re-layouts: 14.3 us -> 0.04 us  [the longest x1 0.02 us: per_device(): layer_out = out_perm.reshape(length, n_core, n_sz, col_w).transpose(0, 2,...]
    all_to_all x1 -> x0, blocking collectives: 13.7 us -> none  [per_device(): lax.all_to_all(out_weight, 'kv', split_axis=0, concat_axis=1, tiled=True)]
    dot_general x8, matrix products: 10.3 us -> 1.86 us  [attend(): lax.dot_general(dscore, query, columns, preferred_element_type=jnp.float32)]
  transfers between devices with their start and end apart: 48 -> 12, of which waited for: 16 -> 9; matrix products, arithmetic and copies ran while one was open for 17% -> 24% of each run, Pallas kernels for 0% -> 0%
where the time goes in v1:
time: 342 us; the launch traced here: 340 us
  waiting for transfers between devices  197 us (58%)
  matrix products  52.4 us (15%)
  starting transfers between devices  33.2 us (10%)
  local copies, waits for them, and re-layouts  30.9 us (9%)
  between operations  14.8 us (4%)
  other arithmetic  12 us (4%)
    all_gather x1, waiting for transfers between devices, per_device(): w_cols = lax.all_gather(out_weight, 'sz', axis=1, tiled=True)  138 us
    reduce_scatter x1, waiting for transfers between devices, per_device(): lax.psum_scatter(hg_part.astype(jnp.bfloat16), 'kv', scatter_dimension=1,...  35.4 us
    ppermute x8, starting transfers between devices, shifted(): return lax.ppermute(block, SEQ, route)  32.8 us
    all_gather x1, local copies, waits for them, and re-layouts, per_device(): w_cols = lax.all_gather(w_cols, 'core', axis=1, tiled=True)  22.5 us
    ppermute x8, waiting for transfers between devices, shifted(): return lax.ppermute(block, SEQ, route)  14.2 us
    dot_general x1, matrix products, per_device(): lax.dot_general(og_perm, w_cols, contract, preferred_element_type=jnp.flo...  11.7 us
    dot_general x8, matrix products, attend(): lax.dot_general(query, key_win, contract, preferred_element_type=jnp.floa...  10.2 us
    dot_general x1, matrix products, per_device(): jnp.einsum('tgr,grc->gtc', attn_all.reshape(length, kv_count, rows), w_co...  8.9 us
  transfers between devices with their start and end apart: 12, of which 9 were waited for; matrix products, arithmetic and copies ran while one was open for 24% of the time, Pallas kernels for 0%

profile of v1, /device:TPU:97, one launch (start us, length us, event | category | flops | bytes accessed | tf_op | source)
XLA Modules:
  0.0 340.2 jit_solution(9585859972369785036)
XLA Ops:
  7.9 138.4 %all-gather.6.cloned.1.call-done = bf16[8192,512]{0,1:T(8,128)(2,1)} async-done(((bf16[8192,32]{0,1:T(8,128)(2,1)}), bf16[8192,512]{0,1:T(8,128)(2,1)}) %all-gather.6.cloned.1.call-update) | async-done | bytes 8388624 | tf_op jit(solution)/shard_map/all_gather | solution.py:130
  148.9 3.5 %collective-permute-start = (bf16[1,129,256]{2,1,0:T(8,128)(2,1)S(1)}, bf16[1,129,256]{2,1,0:T(8,128)(2,1)S(1)}, u32[]{:S(2)}, u32[]{:S(2)}) collective-permute-start(bf16[1,129,256]{2,1,0:T(8,128)(2,1)S(1)} %fusion.55), channel_id=1, source_target_pairs={{0,8},{8,16},{16,24},{24,32},{32,40},{40,48},{48,56},{56,64},{64,7... | collective-permute-start | bytes 198152 | tf_op jit(solution)/shard_map/ppermute | solution.py:30
  154.1 4.7 %collective-permute-start.2 = (bf16[2,129,256]{2,1,0:T(8,128)(2,1)S(1)}, bf16[2,129,256]{2,1,0:T(8,128)(2,1)S(1)}, u32[]{:S(2)}, u32[]{:S(2)}) collective-permute-start(bf16[2,129,256]{2,1,0:T(8,128)(2,1)S(1)} %pad_maximum_fusion.4), channel_id=1, source_target_pairs={{0,16},{8,24},{16,32},{24,40},{32,48},{40,56},{48,64},{56,72},{64,... | collective-permute-start | bytes 396296 | tf_op jit(solution)/shard_map/ppermute | solution.py:30
  158.9 3.1 collective-permute-start.1
  162.4 3.5 %collective-permute-start.3 = (bf16[4,129,256]{2,1,0:T(8,128)(2,1)S(1)}, bf16[4,129,256]{2,1,0:T(8,128)(2,1)S(1)}, u32[]{:S(2)}, u32[]{:S(2)}) collective-permute-start(bf16[4,129,256]{2,1,0:T(8,128)(2,1)S(1)} %pad_maximum_fusion.1), channel_id=1, source_target_pairs={{0,32},{8,40},{16,48},{24,56},{32,64},{40,72},{48,80},{56,88},{64,... | collective-permute-start | bytes 792584 | tf_op jit(solution)/shard_map/ppermute | solution.py:30
  166.6 2.8 collective-permute-done.1
  169.4 3.5 %collective-permute-done.3 = bf16[4,129,256]{2,1,0:T(8,128)(2,1)S(1)} collective-permute-done((bf16[4,129,256]{2,1,0:T(8,128)(2,1)S(1)}, bf16[4,129,256]{2,1,0:T(8,128)(2,1)S(1)}, u32[]{:S(2)}, u32[]{:S(2)}) %collective-permute-start.3) | collective-permute-done | bytes 264224 | tf_op jit(solution)/shard_map/ppermute | solution.py:30
  173.4 1.3 fusion.106
  174.9 1.3 fusion.107
  176.4 1.3 fusion.108
  178.0 1.3 fusion.109
  179.5 1.3 fusion.110
  181.0 1.3 fusion.111
  182.6 1.3 fusion.112
  184.1 1.3 fusion.113
  185.9 0.9 constant_dynamic-update-slice_fusion.12
  187.0 0.9 constant_dynamic-update-slice_fusion.11
  188.2 0.9 constant_dynamic-update-slice_fusion.10
  189.3 0.9 constant_dynamic-update-slice_fusion.9
  190.5 0.9 constant_dynamic-update-slice_fusion.8
  191.7 0.9 constant_dynamic-update-slice_fusion.7
  192.8 0.9 constant_dynamic-update-slice_fusion.6
  194.0 0.9 constant_dynamic-update-slice_fusion.5
  196.1 11.7 %convolution_convert_fusion = bf16[128,8192]{0,1:T(8,128)(2,1)} fusion(bf16[128,1024]{0,1:T(8,128)(2,1)S(1)} %bitcast.186, bf16[8192,1024]{0,1:T(8,128)(2,1)} %all-gather.8.cloned.1.call-done), kind=kOutput, calls=%fused_computation | convolution fusion | flops 2148532224 | bytes 19136512 | tf_op jit(solution)/shard_map/dot_general | solution.py:138
  207.8 22.5 %copy.33 = bf16[8192,1024]{1,0:T(8,128)(2,1)} copy(bf16[8192,1024]{0,1:T(8,128)(2,1)} %all-gather.8.cloned.1.call-done) | data formatting | bytes 33554432 | tf_op jit(solution)/shard_map/all_gather | solution.py:131
  230.3 8.3 %all-gather.4.cloned.1.call-done = bf16[128,8192]{0,1:T(8,128)(2,1)} async-done(((bf16[128,1024]{0,1:T(8,128)(2,1)}), bf16[128,8192]{0,1:T(8,128)(2,1)}) %all-gather.4.cloned.1.call-update) | async-done | bytes 2097168 | tf_op jit(solution)/shard_map/all_gather | solution.py:176
  238.6 8.9 %convolution_convert_fusion.1 = bf16[8,128,1024]{2,1,0:T(8,128)(2,1)S(1)} fusion(bf16[128,8,1024]{0,2,1:T(8,128)(2,1)} %bitcast.183, bf16[8,1024,1024]{2,1,0:T(8,128)(2,1)} %bitcast.166), kind=kOutput, calls=%fused_computation.56 | convolution fusion | flops 2148532224 | bytes 20971520 | tf_op jit(solution)/shard_map/tgr,grc->gtc/dot_general | solution.py:179
  247.5 1.1 reduce_sum.164
  248.6 1.2 copy.35
  249.8 0.9 copy.43
  250.7 35.4 %reduce-scatter.2.cloned.1.call-done = bf16[128,1024]{0,1:T(8,128)(2,1)} async-done(((bf16[128,8192]{0,1:T(8,128)(2,1)}), bf16[128,1024]{0,1:T(8,128)(2,1)}) %reduce-scatter.2.cloned.1.call-update) | async-done | bytes 262160 | tf_op jit(solution)/shard_map/reduce_scatter | solution.py:139
  286.1 1.1 multiply_reduce_fusion
  287.2 1.0 fusion.17
  295.0 0.9 fusion.41
  296.8 2.1 collective-permute-start.4
  299.8 2.4 collective-permute-start.6
  302.2 0.9 fusion.39
  303.1 0.9 fusion.37
  304.1 0.9 fusion.35
  305.0 0.9 fusion.33
  305.9 0.9 fusion.31
  306.9 0.9 fusion.29
  307.8 0.9 fusion.27
  308.8 4.1 %collective-permute-start.5 = (bf16[2,128,256]{2,1,0:T(8,128)(2,1)S(1)}, bf16[2,128,256]{2,1,0:T(8,128)(2,1)S(1)}, u32[]{:S(2)}, u32[]{:S(2)}) collective-permute-start(bf16[2,128,256]{2,1,0:T(8,128)(2,1)S(1)} %slice.350), channel_id=1, source_target_pairs={{16,0},{24,8},{32,16},{40,24},{48,32},{56,40},{64,48},{72,56},{80,... | collective-permute-start | bytes 393224 | tf_op jit(solution)/shard_map/ppermute | solution.py:30
  313.0 1.1 subtract_convert_fusion
  314.1 2.0 collective-permute-done.5
  316.1 9.5 %collective-permute-start.7 = (bf16[1,128,256]{2,1,0:T(8,128)(2,1)S(1)}, bf16[1,128,256]{2,1,0:T(8,128)(2,1)S(1)}, u32[]{:S(2)}, u32[]{:S(2)}) collective-permute-start(bf16[1,128,256]{2,1,0:T(8,128)(2,1)S(1)} %slice.351), channel_id=1, source_target_pairs={{8,0},{16,8},{24,16},{32,24},{40,32},{48,40},{56,48},{64,56},{72,6... | collective-permute-start | bytes 196616 | tf_op jit(solution)/shard_map/ppermute | solution.py:30
  326.5 5.4 %collective-permute-done.7 = bf16[1,128,256]{2,1,0:T(8,128)(2,1)S(1)} collective-permute-done((bf16[1,128,256]{2,1,0:T(8,128)(2,1)S(1)}, bf16[1,128,256]{2,1,0:T(8,128)(2,1)S(1)}, u32[]{:S(2)}, u32[]{:S(2)}) %collective-permute-start.7) | collective-permute-done | bytes 65568 | tf_op jit(solution)/shard_map/ppermute | solution.py:30
  (171 shorter events, 22.2 us)
Async XLA Ops:
  7.2 139.2 %all-gather.6.cloned.1.call-start = ((), (), s32[]{:S(2)}) async-start(), calls=%async_computation.2 | async-start | bytes 8912896 | tf_op jit(solution)/shard_map/all_gather | solution.py:130
  7.9 188.2 %all-gather.8.cloned.1.call-start = ((), (), s32[]{:S(2)}) async-start(), calls=%async_computation.3 | async-start | bytes 25165824 | tf_op jit(solution)/shard_map/all_gather | solution.py:131
  146.4 0.7 copy-start.32
  146.4 1.4 copy-start.34
  146.4 2.1 copy-start.25
  146.4 2.5 copy-start.23
  146.4 6.0 %copy-start.21 = (bf16[128,1024]{1,0:T(8,128)(2,1)S(1)}, bf16[128,1024]{1,0:T(8,128)(2,1)}, u32[]{:S(2)}) copy-start(bf16[128,1024]{1,0:T(8,128)(2,1)} %param.10) | copy-start | bytes 786436
  146.4 6.2 %copy-start.33 = (s32[1,32]{1,0:T(1,128)S(1)}, s32[1,32]{1,0:T(1,128)}, u32[]{:S(2)}) copy-start(s32[1,32]{1,0:T(1,128)} %param.16) | copy-start | bytes 388
  146.4 92.2 %all-gather.4.cloned.1.call-start = ((), (), s32[]{:S(2)}) async-start(), calls=%async_computation.1 | async-start | bytes 2359296 | tf_op jit(solution)/shard_map/all_gather | solution.py:176
  147.7 25.3 %copy-start.26 = (f32[64]{0:T(128)}, f32[64]{0:T(128)S(1)}, u32[]{:S(2)}) copy-start(f32[64]{0:T(128)S(1)} %multiply_exponential_fusion) | copy-start | bytes 772
  147.7 25.3 %copy-start.28 = (pred[64]{0:T(512)(128)(4,1)}, pred[64]{0:T(512)(128)(4,1)S(1)}, u32[]{:S(2)}) copy-start(pred[64]{0:T(512)(128)(4,1)S(1)} %get-tuple-element.84) | copy-start | bytes 196
  147.8 25.3 %copy-start.30 = (pred[64]{0:T(512)(128)(4,1)}, pred[64]{0:T(512)(128)(4,1)S(1)}, u32[]{:S(2)}) copy-start(pred[64]{0:T(512)(128)(4,1)S(1)} %get-tuple-element.85) | copy-start | bytes 196
  148.9 4.8 %collective-permute-start = (bf16[1,129,256]{2,1,0:T(8,128)(2,1)S(1)}, bf16[1,129,256]{2,1,0:T(8,128)(2,1)S(1)}, u32[]{:S(2)}, u32[]{:S(2)}) collective-permute-start(bf16[1,129,256]{2,1,0:T(8,128)(2,1)S(1)} %fusion.55), channel_id=1, source_target_pairs={{0,8},{8,16},{16,24},{24,32},{32,40},{40,48},{48,56},{56,64},{64,7... | collective-permute-start | bytes 198152 | tf_op jit(solution)/shard_map/ppermute | solution.py:30
  153.5 0.6 copy-start.19
  154.1 8.2 %collective-permute-start.2 = (bf16[2,129,256]{2,1,0:T(8,128)(2,1)S(1)}, bf16[2,129,256]{2,1,0:T(8,128)(2,1)S(1)}, u32[]{:S(2)}, u32[]{:S(2)}) collective-permute-start(bf16[2,129,256]{2,1,0:T(8,128)(2,1)S(1)} %pad_maximum_fusion.4), channel_id=1, source_target_pairs={{0,16},{8,24},{16,32},{24,40},{32,48},{40,56},{48,64},{56,72},{64,... | collective-permute-start | bytes 396296 | tf_op jit(solution)/shard_map/ppermute | solution.py:30
  158.9 10.6 %collective-permute-start.1 = (bf16[2,129,256]{2,1,0:T(8,128)(2,1)S(1)}, bf16[2,129,256]{2,1,0:T(8,128)(2,1)S(1)}, u32[]{:S(2)}, u32[]{:S(2)}) collective-permute-start(bf16[2,129,256]{2,1,0:T(8,128)(2,1)S(1)} %pad_maximum_fusion.4), channel_id=1, source_target_pairs={{0,64},{8,72},{16,80},{24,88},{32,96},{40,104},{48,112},{56,120},{... | collective-permute-start | bytes 396296 | tf_op jit(solution)/shard_map/ppermute | solution.py:30
  162.4 10.6 %collective-permute-start.3 = (bf16[4,129,256]{2,1,0:T(8,128)(2,1)S(1)}, bf16[4,129,256]{2,1,0:T(8,128)(2,1)S(1)}, u32[]{:S(2)}, u32[]{:S(2)}) collective-permute-start(bf16[4,129,256]{2,1,0:T(8,128)(2,1)S(1)} %pad_maximum_fusion.1), channel_id=1, source_target_pairs={{0,32},{8,40},{16,48},{24,56},{32,64},{40,72},{48,80},{56,88},{64,... | collective-permute-start | bytes 792584 | tf_op jit(solution)/shard_map/ppermute | solution.py:30
  185.9 3.4 %copy-start.10 = (bf16[128,1280]{1,0:T(8,128)(2,1)}, bf16[128,1280]{1,0:T(8,128)(2,1)S(1)}, u32[]{:S(2)}) copy-start(bf16[128,1280]{1,0:T(8,128)(2,1)S(1)} %divide_convert_fusion.7) | copy-start | bytes 983044
  189.3 3.5 %copy-start = (bf16[128,1280]{1,0:T(8,128)(2,1)}, bf16[128,1280]{1,0:T(8,128)(2,1)S(1)}, u32[]{:S(2)}) copy-start(bf16[128,1280]{1,0:T(8,128)(2,1)S(1)} %divide_convert_fusion.4) | copy-start | bytes 983044
  190.5 3.5 %copy-start.2 = (bf16[128,1280]{1,0:T(8,128)(2,1)}, bf16[128,1280]{1,0:T(8,128)(2,1)S(1)}, u32[]{:S(2)}) copy-start(bf16[128,1280]{1,0:T(8,128)(2,1)S(1)} %divide_convert_fusion.3) | copy-start | bytes 983044
  191.6 4.0 %copy-start.4 = (bf16[128,1280]{1,0:T(8,128)(2,1)}, bf16[128,1280]{1,0:T(8,128)(2,1)S(1)}, u32[]{:S(2)}) copy-start(bf16[128,1280]{1,0:T(8,128)(2,1)S(1)} %divide_convert_fusion.2) | copy-start | bytes 983044
  191.6 4.2 %copy-start.22 = (bf16[128,1024]{1,0:T(8,128)(2,1)S(1)}, bf16[128,1024]{1,0:T(8,128)(2,1)}, u32[]{:S(2)}) copy-start(bf16[128,1024]{1,0:T(8,128)(2,1)} %param.14) | copy-start | bytes 786436
  192.8 15.0 %copy-start.6 = (bf16[128,1280]{1,0:T(8,128)(2,1)}, bf16[128,1280]{1,0:T(8,128)(2,1)S(1)}, u32[]{:S(2)}) copy-start(bf16[128,1280]{1,0:T(8,128)(2,1)S(1)} %divide_convert_fusion.1) | copy-start | bytes 983044
  194.0 13.8 %copy-start.8 = (bf16[128,1280]{1,0:T(8,128)(2,1)}, bf16[128,1280]{1,0:T(8,128)(2,1)S(1)}, u32[]{:S(2)}) copy-start(bf16[128,1280]{1,0:T(8,128)(2,1)S(1)} %divide_convert_fusion) | copy-start | bytes 983044
  194.9 0.7 copy-start.18
  195.7 90.4 %reduce-scatter.2.cloned.1.call-start = ((), (), s32[]{:S(2)}) async-start(), calls=%async_computation.4 | async-start | bytes 2359296 | tf_op jit(solution)/shard_map/reduce_scatter | solution.py:139
  248.6 38.6 %copy-start.11 = (bf16[128,1280]{1,0:T(8,128)(2,1)S(1)}, bf16[128,1280]{1,0:T(8,128)(2,1)}, u32[]{:S(2)}) copy-start(bf16[128,1280]{1,0:T(8,128)(2,1)} %copy-done.10) | copy-start | bytes 983044
  248.6 39.7 %copy-start.17 = (bf16[128,8,128]{0,2,1:T(8,128)(2,1)S(1)}, bf16[128,8,128]{0,2,1:T(8,128)(2,1)}, u32[]{:S(2)}) copy-start(bf16[128,8,128]{0,2,1:T(8,128)(2,1)} %pad_maximum_fusion.2) | copy-start | bytes 786436
  286.1 2.4 copy-start.16
  288.8 1.0 copy-start.1
  289.3 1.0 copy-start.3
  290.1 1.0 copy-start.5
  290.6 1.0 copy-start.7
  291.3 1.0 copy-start.9
  291.9 1.0 copy-start.12
  292.6 0.7 copy-start.14
  296.8 12.0 %collective-permute-start.4 = (bf16[4,128,256]{2,1,0:T(8,128)(2,1)}, bf16[4,128,256]{2,1,0:T(8,128)(2,1)S(1)}, u32[]{:S(2)}, u32[]{:S(2)}) collective-permute-start(bf16[4,128,256]{2,1,0:T(8,128)(2,1)} %bitcast.33), channel_id=1, source_target_pairs={{32,0},{40,8},{48,16},{56,24},{64,32},{72,40},{80,48},{88,56},{96,... | collective-permute-start | bytes 786440 | tf_op jit(solution)/shard_map/ppermute | solution.py:30
  299.0 7.8 %copy-start.13 = (bf16[128,1280]{1,0:T(8,128)(2,1)S(1)}, bf16[128,1280]{1,0:T(8,128)(2,1)}, u32[]{:S(2)}) copy-start(bf16[128,1280]{1,0:T(8,128)(2,1)} %copy-done.12) | copy-start | bytes 983044
  299.8 8.0 %copy-start.15 = (bf16[128,1280]{1,0:T(8,128)(2,1)S(1)}, bf16[128,1280]{1,0:T(8,128)(2,1)}, u32[]{:S(2)}) copy-start(bf16[128,1280]{1,0:T(8,128)(2,1)} %copy-done.14) | copy-start | bytes 983044
  299.8 14.3 %collective-permute-start.6 = (bf16[2,128,256]{2,1,0:T(8,128)(2,1)}, bf16[2,128,256]{2,1,0:T(8,128)(2,1)S(1)}, u32[]{:S(2)}, u32[]{:S(2)}) collective-permute-start(bf16[2,128,256]{2,1,0:T(8,128)(2,1)} %bitcast.207), channel_id=1, source_target_pairs={{64,0},{72,8},{80,16},{88,24},{96,32},{104,40},{112,48},{120,56},{... | collective-permute-start | bytes 393224 | tf_op jit(solution)/shard_map/ppermute | solution.py:30
  305.0 8.0 %copy-start.20 = (f32[128,64]{0,1:T(8,128)S(1)}, f32[128,64]{0,1:T(8,128)}, u32[]{:S(2)}) copy-start(f32[128,64]{0,1:T(8,128)} %copy-done.19) | copy-start | bytes 98308
  305.0 8.0 %copy-start.24 = (f32[128,64]{0,1:T(8,128)S(1)}, f32[128,64]{0,1:T(8,128)}, u32[]{:S(2)}) copy-start(f32[128,64]{0,1:T(8,128)} %get-tuple-element.46) | copy-start | bytes 98308
  308.8 23.8 %copy-start.27 = (f32[64]{0:T(128)S(1)}, f32[64]{0:T(128)}, u32[]{:S(2)}) copy-start(f32[64]{0:T(128)} %copy-done.26) | copy-start | bytes 772
  308.8 23.8 %copy-start.29 = (pred[64]{0:T(512)(128)(4,1)S(1)}, pred[64]{0:T(512)(128)(4,1)}, u32[]{:S(2)}) copy-start(pred[64]{0:T(512)(128)(4,1)} %copy-done.28) | copy-start | bytes 196
  308.8 23.8 %copy-start.31 = (pred[64]{0:T(512)(128)(4,1)S(1)}, pred[64]{0:T(512)(128)(4,1)}, u32[]{:S(2)}) copy-start(pred[64]{0:T(512)(128)(4,1)} %copy-done.30) | copy-start | bytes 196
  308.8 7.2 %collective-permute-start.5 = (bf16[2,128,256]{2,1,0:T(8,128)(2,1)S(1)}, bf16[2,128,256]{2,1,0:T(8,128)(2,1)S(1)}, u32[]{:S(2)}, u32[]{:S(2)}) collective-permute-start(bf16[2,128,256]{2,1,0:T(8,128)(2,1)S(1)} %slice.350), channel_id=1, source_target_pairs={{16,0},{24,8},{32,16},{40,24},{48,32},{56,40},{64,48},{72,56},{80,... | collective-permute-start | bytes 393224 | tf_op jit(solution)/shard_map/ppermute | solution.py:30
  316.1 15.8 %collective-permute-start.7 = (bf16[1,128,256]{2,1,0:T(8,128)(2,1)S(1)}, bf16[1,128,256]{2,1,0:T(8,128)(2,1)S(1)}, u32[]{:S(2)}, u32[]{:S(2)}) collective-permute-start(bf16[1,128,256]{2,1,0:T(8,128)(2,1)S(1)} %slice.351), channel_id=1, source_target_pairs={{8,0},{16,8},{24,16},{32,24},{40,32},{48,40},{56,48},{64,56},{72,6... | collective-permute-start | bytes 196616 | tf_op jit(solution)/shard_map/ppermute | solution.py:30
Sparse Core Ops, SparseCore 0:
  10.6 135.7 all-gather.5
  148.2 33.9 all-gather.7
  195.8 42.7 all-gather.3
  241.0 45.0 reduce-scatter.1

commit v2 on v1

--- a/solution.py
+++ b/solution.py
@@ -126,14 +126,8 @@
         .astype(jnp.bfloat16)
         .reshape(length, groups * HD)
     )
-    col_w = out_weight.shape[1]
-    w_cols = lax.all_gather(out_weight, "sz", axis=1, tiled=True)
-    w_cols = lax.all_gather(w_cols, "core", axis=1, tiled=True)
-    og_perm = (
-        out_grad.reshape(length, n_sz, n_core, col_w)
-        .transpose(0, 2, 1, 3)
-        .reshape(length, n_sz * n_core * col_w)
-    )
+    w_cols = lax.all_gather(out_weight, SEQ, axis=1, tiled=True)
+    og_perm = out_grad
     contract = (((1,), (1,)), ((), ()))
     hg_part = lax.dot_general(og_perm, w_cols, contract, preferred_element_type=jnp.float32)
     head_grad = lax.psum_scatter(
@@ -173,22 +167,22 @@
         dvalue_sum = dvalue_sum + dvalue
     attn = jnp.concatenate(outputs, axis=1)
     dq_rot = jnp.stack(dqueries, axis=1)
-    attn_all = lax.all_gather(attn, "kv", axis=1, tiled=True)
     kv_count = lax.axis_size("kv")
+    kv_me = lax.axis_index("kv")
     rows = attn.shape[1]
-    parts = jnp.einsum(
-        "tgr,grc->gtc",
-        attn_all.reshape(length, kv_count, rows),
-        w_cols.reshape(kv_count, rows, -1),
-        preferred_element_type=jnp.float32,
-    ).astype(jnp.bfloat16)
-    parts = lax.optimization_barrier(parts)
-    out_perm = jnp.sum(parts.astype(jnp.float32), axis=0).astype(jnp.bfloat16)
-    layer_out = (
-        out_perm.reshape(length, n_core, n_sz, col_w)
-        .transpose(0, 2, 1, 3)
-        .reshape(length, n_sz * n_core * col_w)
-    )
+    total = None
+    for step in range(kv_count):
+        if step == 0:
+            piece = attn
+        else:
+            route = [(i, (i + step) % kv_count) for i in range(kv_count)]
+            piece = lax.ppermute(attn, "kv", route)
+        src = (kv_me - step) % kv_count
+        w_rows = lax.dynamic_slice_in_dim(w_cols, src * rows, rows, 0)
+        part = jnp.dot(piece, w_rows, preferred_element_type=jnp.float32).astype(jnp.bfloat16)
+        part = lax.optimization_barrier(part)
+        total = part.astype(jnp.float32) if total is None else total + part.astype(jnp.float32)
+    layer_out = total.astype(jnp.bfloat16)
     dkv = jnp.concatenate([dkey_sum, dvalue_sum], axis=1).reshape(REACH + 1, length, 2 * HD)
     dkv_total = return_window(dkv)
     dk_total = dkv_total[:, :HD]

time: 342 us -> 288 us (0.84)
  waiting for transfers between devices: 197 us -> 134 us
  local copies, waits for them, and re-layouts: 30.9 us -> 5.76 us
  starting transfers between devices: 33.2 us -> 45.8 us
  matrix products: 52.4 us -> 64.5 us
  other arithmetic: 12 us -> 18.8 us
    all_gather x3 -> x1, waiting for transfers between devices: 147 us -> 88.3 us  [per_device(): w_cols = lax.all_gather(out_weight, SEQ, axis=1, tiled=True)]
    reduce_scatter x1, waiting for transfers between devices: 35.4 us -> 5.68 us  [per_device(): lax.psum_scatter(hg_part.astype(jnp.bfloat16), 'kv', scatter_dimension=1,...]
    all_gather x1 -> x0, local copies, waits for them, and re-layouts: 22.5 us -> none  [per_device(): w_cols = lax.all_gather(w_cols, 'core', axis=1, tiled=True)]
    ppermute x0 -> x7, waiting for transfers between devices: none -> 17.1 us  [per_device(): piece = lax.ppermute(attn, 'kv', route)]
    ppermute x0 -> x7, starting transfers between devices: none -> 11.7 us  [per_device(): piece = lax.ppermute(attn, 'kv', route)]
    dot_general x1 -> x8, matrix products: 8.9 us -> 19.7 us  [per_device(): jnp.dot(piece, w_rows, preferred_element_type=jnp.float32)]
    ppermute x8, waiting for transfers between devices: 14.2 us -> 22.6 us  [shifted(): return lax.ppermute(block, SEQ, route)]
  transfers between devices with their start and end apart: 12 -> 17, of which waited for: 9 -> 10; matrix products, arithmetic and copies ran while one was open for 24% -> 22% of each run, Pallas kernels for 0% -> 0%
where the time goes in v2:
time: 288 us; the launch traced here: 284 us
  waiting for transfers between devices  134 us (47%)
  matrix products  64.5 us (22%)
  starting transfers between devices  45.8 us (16%)
  other arithmetic  18.8 us (7%)
  between operations  15.1 us (5%)
  local copies, waits for them, and re-layouts  5.76 us (2%)
    all_gather x1, waiting for transfers between devices, per_device(): w_cols = lax.all_gather(out_weight, SEQ, axis=1, tiled=True)  88.3 us
    ppermute x8, starting transfers between devices, shifted(): return lax.ppermute(block, SEQ, route)  34 us
    ppermute x8, waiting for transfers between devices, shifted(): return lax.ppermute(block, SEQ, route)  22.6 us
    dot_general x8, matrix products, per_device(): jnp.dot(piece, w_rows, preferred_element_type=jnp.float32)  19.7 us
    ppermute x7, waiting for transfers between devices, per_device(): piece = lax.ppermute(attn, 'kv', route)  17.1 us
    ppermute x7, starting transfers between devices, per_device(): piece = lax.ppermute(attn, 'kv', route)  11.7 us
    dot_general x1, matrix products, per_device(): lax.dot_general(og_perm, w_cols, contract, preferred_element_type=jnp.flo...  11.7 us
    dot_general x8, matrix products, attend(): lax.dot_general(query, key_win, contract, preferred_element_type=jnp.floa...  10.8 us
  transfers between devices with their start and end apart: 17, of which 10 were waited for; matrix products, arithmetic and copies ran while one was open for 22% of the time, Pallas kernels for 0%

profile of v2, /device:TPU:97, one launch (start us, length us, event | category | flops | bytes accessed | tf_op | source)
XLA Modules:
  0.0 284.4 jit_solution(191662761755855573)
XLA Ops:
  9.3 1.3 fusion.152
  12.6 5.2 %collective-permute-start = (bf16[1,129,256]{2,1,0:T(8,128)(2,1)S(1)}, bf16[1,129,256]{2,1,0:T(8,128)(2,1)S(1)}, u32[]{:S(2)}, u32[]{:S(2)}) collective-permute-start(bf16[1,129,256]{2,1,0:T(8,128)(2,1)S(1)} %fusion.95), channel_id=1, source_target_pairs={{0,8},{8,16},{16,24},{24,32},{32,40},{40,48},{48,56},{56,64},{64,7... | collective-permute-start | bytes 198152 | tf_op jit(solution)/shard_map/ppermute | solution.py:30
  17.9 1.1 copy.12
  20.8 4.7 %collective-permute-start.2 = (bf16[2,129,256]{2,1,0:T(8,128)(2,1)S(1)}, bf16[2,129,256]{2,1,0:T(8,128)(2,1)S(1)}, u32[]{:S(2)}, u32[]{:S(2)}) collective-permute-start(bf16[2,129,256]{2,1,0:T(8,128)(2,1)S(1)} %pad_maximum_fusion.4), channel_id=1, source_target_pairs={{0,16},{8,24},{16,32},{24,40},{32,48},{40,56},{48,64},{56,72},{64,... | collective-permute-start | bytes 396296 | tf_op jit(solution)/shard_map/ppermute | solution.py:30
  25.5 3.1 %collective-permute-start.1 = (bf16[2,129,256]{2,1,0:T(8,128)(2,1)S(1)}, bf16[2,129,256]{2,1,0:T(8,128)(2,1)S(1)}, u32[]{:S(2)}, u32[]{:S(2)}) collective-permute-start(bf16[2,129,256]{2,1,0:T(8,128)(2,1)S(1)} %pad_maximum_fusion.4), channel_id=1, source_target_pairs={{0,64},{8,72},{16,80},{24,88},{32,96},{40,104},{48,112},{56,120},{... | collective-permute-start | bytes 396296 | tf_op jit(solution)/shard_map/ppermute | solution.py:30
  28.6 2.7 collective-permute-done.2
  31.4 6.0 %collective-permute-start.3 = (bf16[4,129,256]{2,1,0:T(8,128)(2,1)S(1)}, bf16[4,129,256]{2,1,0:T(8,128)(2,1)S(1)}, u32[]{:S(2)}, u32[]{:S(2)}) collective-permute-start(bf16[4,129,256]{2,1,0:T(8,128)(2,1)S(1)} %pad_maximum_fusion.1), channel_id=1, source_target_pairs={{0,32},{8,40},{16,48},{24,56},{32,64},{40,72},{48,80},{56,88},{64,... | collective-permute-start | bytes 792584 | tf_op jit(solution)/shard_map/ppermute | solution.py:30
  38.9 10.6 %collective-permute-done.3 = bf16[4,129,256]{2,1,0:T(8,128)(2,1)S(1)} collective-permute-done((bf16[4,129,256]{2,1,0:T(8,128)(2,1)S(1)}, bf16[4,129,256]{2,1,0:T(8,128)(2,1)S(1)}, u32[]{:S(2)}, u32[]{:S(2)}) %collective-permute-start.3) | collective-permute-done | bytes 264224 | tf_op jit(solution)/shard_map/ppermute | solution.py:30
  49.9 1.3 fusion.154
  51.4 1.3 fusion.155
  52.9 1.3 fusion.156
  54.4 1.3 fusion.157
  56.0 1.3 fusion.158
  57.5 1.3 fusion.159
  59.1 1.3 fusion.160
  68.5 1.9 fusion.161
  70.6 88.3 %all-gather.2.cloned.1.call-done = bf16[8192,1024]{0,1:T(8,128)(2,1)} async-done(((bf16[8192,32]{0,1:T(8,128)(2,1)}), bf16[8192,1024]{0,1:T(8,128)(2,1)}) %all-gather.2.cloned.1.call-update) | async-done | bytes 16777232 | tf_op jit(solution)/shard_map/all_gather | solution.py:129
  158.9 11.7 %convolution_convert_fusion = bf16[128,8192]{0,1:T(8,128)(2,1)} fusion(bf16[128,1024]{1,0:T(8,128)(2,1)S(1)} %copy-done, bf16[8192,1024]{0,1:T(8,128)(2,1)} %all-gather.2.cloned.1.call-done), kind=kOutput, calls=%fused_computation | convolution fusion | flops 2148532224 | bytes 19136512 | tf_op jit(solution)/shard_map/dot_general | solution.py:132
  172.5 1.3 divide_convert_fusion.1
  175.9 1.2 collective-permute-start.4
  177.1 2.4 collective-permute-start.5
  179.5 1.2 collective-permute-start.6
  180.7 1.2 collective-permute-start.7
  182.2 12.0 %collective-permute-done.4 = bf16[128,1024]{0,1:T(8,128)(2,1)} collective-permute-done((bf16[128,1024]{0,1:T(8,128)(2,1)}, bf16[128,1024]{0,1:T(8,128)(2,1)}, u32[]{:S(2)}, u32[]{:S(2)}) %collective-permute-start.4) | collective-permute-done | bytes 262176 | tf_op jit(solution)/shard_map/ppermute | solution.py:179
  194.2 2.5 fusion.45
  196.8 2.6 collective-permute-done.5
  199.3 5.4 %collective-permute-start.10 = (bf16[128,1024]{0,1:T(8,128)(2,1)S(1)}, bf16[128,1024]{0,1:T(8,128)(2,1)S(1)}, u32[]{:S(2)}, u32[]{:S(2)}) collective-permute-start(bf16[128,1024]{0,1:T(8,128)(2,1)S(1)} %copy-done.21), channel_id=1, source_target_pairs={{0,7},{1,0},{2,1},{3,2},{4,3},{5,4},{6,5},{7,6},{8,15},{9,8},{10,9... | collective-permute-start | bytes 786440 | tf_op jit(solution)/shard_map/ppermute | solution.py:179
  204.7 2.5 fusion.48
  207.3 2.5 fusion.51
  209.8 2.5 fusion.54
  212.2 2.5 collective-permute-done.8
  214.7 2.4 fusion.57
  217.2 2.4 fusion.60
  219.6 2.4 fusion.63
  222.1 2.4 fusion.42
  224.5 1.1 add_convert_fusion
  225.6 5.7 %reduce-scatter.2.cloned.1.call-done = bf16[128,1024]{0,1:T(8,128)(2,1)} async-done(((bf16[128,8192]{0,1:T(8,128)(2,1)}), bf16[128,1024]{0,1:T(8,128)(2,1)}) %reduce-scatter.2.cloned.1.call-update) | async-done | bytes 262160 | tf_op jit(solution)/shard_map/reduce_scatter | solution.py:133
  231.2 1.1 multiply_reduce_fusion
  232.4 1.0 fusion.17
  233.4 1.0 fusion.119
  242.1 2.0 collective-permute-start.11
  244.5 3.1 %collective-permute-start.13 = (bf16[2,128,256]{2,1,0:T(8,128)(2,1)S(1)}, bf16[2,128,256]{2,1,0:T(8,128)(2,1)S(1)}, u32[]{:S(2)}, u32[]{:S(2)}) collective-permute-start(bf16[2,128,256]{2,1,0:T(8,128)(2,1)S(1)} %bitcast.197), channel_id=1, source_target_pairs={{64,0},{72,8},{80,16},{88,24},{96,32},{104,40},{112,48},{120,56},{... | collective-permute-start | bytes 393224 | tf_op jit(solution)/shard_map/ppermute | solution.py:30
  254.2 1.0 convert_add_fusion
  255.3 2.5 collective-permute-start.12
  257.7 1.1 subtract_convert_fusion
  258.9 3.6 %collective-permute-done.12 = bf16[2,128,256]{2,1,0:T(8,128)(2,1)S(1)} collective-permute-done((bf16[2,128,256]{2,1,0:T(8,128)(2,1)S(1)}, bf16[2,128,256]{2,1,0:T(8,128)(2,1)S(1)}, u32[]{:S(2)}, u32[]{:S(2)}) %collective-permute-start.12) | collective-permute-done | bytes 131104 | tf_op jit(solution)/shard_map/ppermute | solution.py:30
  262.5 7.5 %collective-permute-start.14 = (bf16[1,128,256]{2,1,0:T(8,128)(2,1)S(1)}, bf16[1,128,256]{2,1,0:T(8,128)(2,1)S(1)}, u32[]{:S(2)}, u32[]{:S(2)}) collective-permute-start(bf16[1,128,256]{2,1,0:T(8,128)(2,1)S(1)} %slice.351), channel_id=1, source_target_pairs={{8,0},{16,8},{24,16},{32,24},{40,32},{48,40},{56,48},{64,56},{72,6... | collective-permute-start | bytes 196616 | tf_op jit(solution)/shard_map/ppermute | solution.py:30
  270.9 4.9 %collective-permute-done.14 = bf16[1,128,256]{2,1,0:T(8,128)(2,1)S(1)} collective-permute-done((bf16[1,128,256]{2,1,0:T(8,128)(2,1)S(1)}, bf16[1,128,256]{2,1,0:T(8,128)(2,1)S(1)}, u32[]{:S(2)}, u32[]{:S(2)}) %collective-permute-start.14) | collective-permute-done | bytes 65568 | tf_op jit(solution)/shard_map/ppermute | solution.py:30
  (190 shorter events, 39.0 us)
Async XLA Ops:
  7.2 151.7 %copy-start = (bf16[128,1024]{1,0:T(8,128)(2,1)S(1)}, bf16[128,1024]{1,0:T(8,128)(2,1)}, u32[]{:S(2)}) copy-start(bf16[128,1024]{1,0:T(8,128)(2,1)} %param.14) | copy-start | bytes 786436
  7.2 151.7 %all-gather.2.cloned.1.call-start = ((), (), s32[]{:S(2)}) async-start(), calls=%async_computation.1 | async-start | bytes 17301504 | tf_op jit(solution)/shard_map/all_gather | solution.py:129
  7.9 223.3 %reduce-scatter.2.cloned.1.call-start = ((), (), s32[]{:S(2)}) async-start(), calls=%async_computation.2 | async-start | bytes 2359296 | tf_op jit(solution)/shard_map/reduce_scatter | solution.py:133
  9.3 11.3 %copy-start.26 = (f32[64]{0:T(128)}, f32[64]{0:T(128)S(1)}, u32[]{:S(2)}) copy-start(f32[64]{0:T(128)S(1)} %multiply_exponential_fusion) | copy-start | bytes 772
  9.3 11.2 %copy-start.28 = (pred[64]{0:T(512)(128)(4,1)}, pred[64]{0:T(512)(128)(4,1)S(1)}, u32[]{:S(2)}) copy-start(pred[64]{0:T(512)(128)(4,1)S(1)} %get-tuple-element.76) | copy-start | bytes 196
  9.3 11.2 %copy-start.30 = (pred[64]{0:T(512)(128)(4,1)}, pred[64]{0:T(512)(128)(4,1)S(1)}, u32[]{:S(2)}) copy-start(pred[64]{0:T(512)(128)(4,1)S(1)} %get-tuple-element.77) | copy-start | bytes 196
  12.6 8.1 %collective-permute-start = (bf16[1,129,256]{2,1,0:T(8,128)(2,1)S(1)}, bf16[1,129,256]{2,1,0:T(8,128)(2,1)S(1)}, u32[]{:S(2)}, u32[]{:S(2)}) collective-permute-start(bf16[1,129,256]{2,1,0:T(8,128)(2,1)S(1)} %fusion.95), channel_id=1, source_target_pairs={{0,8},{8,16},{16,24},{24,32},{32,40},{40,48},{48,56},{56,64},{64,7... | collective-permute-start | bytes 198152 | tf_op jit(solution)/shard_map/ppermute | solution.py:30
  17.9 31.7 %copy-start.24 = (bf16[128,128]{1,0:T(8,128)(2,1)S(1)}, bf16[128,128]{1,0:T(8,128)(2,1)}, u32[]{:S(2)}) copy-start(bf16[128,128]{1,0:T(8,128)(2,1)} %param.12) | copy-start | bytes 98308
  20.6 17.5 %copy-start.22 = (f32[128,64]{0,1:T(8,128)}, f32[128,64]{0,1:T(8,128)S(1)}, u32[]{:S(2)}) copy-start(f32[128,64]{0,1:T(8,128)S(1)} %get-tuple-element.40) | copy-start | bytes 98308
  20.7 29.2 %copy-start.38 = (s32[128]{0:T(128)S(1)}, s32[128]{0:T(128)}, u32[]{:S(2)}) copy-start(s32[128]{0:T(128)} %param.15) | copy-start | bytes 1540
  20.7 38.3 %copy-start.34 = (pred[1280]{0:T(1024)(128)(4,1)}, pred[1280]{0:T(1024)(128)(4,1)S(1)}, u32[]{:S(2)}) copy-start(pred[1280]{0:T(1024)(128)(4,1)S(1)} %broadcast_bitcast_fusion) | copy-start | bytes 3844
  20.8 10.5 %collective-permute-start.2 = (bf16[2,129,256]{2,1,0:T(8,128)(2,1)S(1)}, bf16[2,129,256]{2,1,0:T(8,128)(2,1)S(1)}, u32[]{:S(2)}, u32[]{:S(2)}) collective-permute-start(bf16[2,129,256]{2,1,0:T(8,128)(2,1)S(1)} %pad_maximum_fusion.4), channel_id=1, source_target_pairs={{0,16},{8,24},{16,32},{24,40},{32,48},{40,56},{48,64},{56,72},{64,... | collective-permute-start | bytes 396296 | tf_op jit(solution)/shard_map/ppermute | solution.py:30
  25.5 33.6 %copy-start.36 = (pred[1280]{0:T(1024)(128)(4,1)}, pred[1280]{0:T(1024)(128)(4,1)S(1)}, u32[]{:S(2)}) copy-start(pred[1280]{0:T(1024)(128)(4,1)S(1)} %fusion.141) | copy-start | bytes 3844
  25.5 13.4 %collective-permute-start.1 = (bf16[2,129,256]{2,1,0:T(8,128)(2,1)S(1)}, bf16[2,129,256]{2,1,0:T(8,128)(2,1)S(1)}, u32[]{:S(2)}, u32[]{:S(2)}) collective-permute-start(bf16[2,129,256]{2,1,0:T(8,128)(2,1)S(1)} %pad_maximum_fusion.4), channel_id=1, source_target_pairs={{0,64},{8,72},{16,80},{24,88},{32,96},{40,104},{48,112},{56,120},{... | collective-permute-start | bytes 396296 | tf_op jit(solution)/shard_map/ppermute | solution.py:30
  31.4 18.1 %collective-permute-start.3 = (bf16[4,129,256]{2,1,0:T(8,128)(2,1)S(1)}, bf16[4,129,256]{2,1,0:T(8,128)(2,1)S(1)}, u32[]{:S(2)}, u32[]{:S(2)}) collective-permute-start(bf16[4,129,256]{2,1,0:T(8,128)(2,1)S(1)} %pad_maximum_fusion.1), channel_id=1, source_target_pairs={{0,32},{8,40},{16,48},{24,56},{32,64},{40,72},{48,80},{56,88},{64,... | collective-permute-start | bytes 792584 | tf_op jit(solution)/shard_map/ppermute | solution.py:30
  60.3 4.2 %copy-start.32 = (f32[128]{0:T(128)}, f32[128]{0:T(128)S(1)}, u32[]{:S(2)}) copy-start(f32[128]{0:T(128)S(1)} %get-tuple-element.68) | copy-start | bytes 1540
  64.5 4.0 %copy-start.35 = (pred[1280]{0:T(1024)(128)(4,1)S(1)}, pred[1280]{0:T(1024)(128)(4,1)}, u32[]{:S(2)}) copy-start(pred[1280]{0:T(1024)(128)(4,1)} %copy-done.34) | copy-start | bytes 3844
  64.6 3.9 %copy-start.37 = (pred[1280]{0:T(1024)(128)(4,1)S(1)}, pred[1280]{0:T(1024)(128)(4,1)}, u32[]{:S(2)}) copy-start(pred[1280]{0:T(1024)(128)(4,1)} %copy-done.36) | copy-start | bytes 3844
  64.6 3.9 %copy-start.39 = (s32[128]{0:T(128)S(1)}, s32[128]{0:T(128)}, u32[]{:S(2)}) copy-start(s32[128]{0:T(128)} %param.15) | copy-start | bytes 1540
  70.4 100.2 %copy-start.16 = (f32[128,1280]{1,0:T(8,128)}, f32[128,1280]{1,0:T(8,128)S(1)}, u32[]{:S(2)}) copy-start(f32[128,1280]{1,0:T(8,128)S(1)} %get-tuple-element.73) | copy-start | bytes 1966084
  170.6 4.2 %copy-start.33 = (f32[128]{0:T(128)S(1)}, f32[128]{0:T(128)}, u32[]{:S(2)}) copy-start(f32[128]{0:T(128)} %get-tuple-element.72) | copy-start | bytes 1540
  171.5 3.2 %copy-start.17 = (f32[128,1280]{1,0:T(8,128)S(1)}, f32[128,1280]{1,0:T(8,128)}, u32[]{:S(2)}) copy-start(f32[128,1280]{1,0:T(8,128)} %copy-done.16) | copy-start | bytes 1966084
  175.9 18.3 %collective-permute-start.4 = (bf16[128,1024]{0,1:T(8,128)(2,1)}, bf16[128,1024]{0,1:T(8,128)(2,1)}, u32[]{:S(2)}, u32[]{:S(2)}) collective-permute-start(bf16[128,1024]{0,1:T(8,128)(2,1)} %get-tuple-element.74), channel_id=1, source_target_pairs={{0,1},{1,2},{2,3},{3,4},{4,5},{5,6},{6,7},{7,0},{8,9},{9,10},{10,1... | collective-permute-start | bytes 786440 | tf_op jit(solution)/shard_map/ppermute | solution.py:179
  177.1 22.2 %collective-permute-start.5 = (bf16[128,1024]{0,1:T(8,128)(2,1)}, bf16[128,1024]{0,1:T(8,128)(2,1)}, u32[]{:S(2)}, u32[]{:S(2)}) collective-permute-start(bf16[128,1024]{0,1:T(8,128)(2,1)} %get-tuple-element.74), channel_id=1, source_target_pairs={{0,2},{1,3},{2,4},{3,5},{4,6},{5,7},{6,0},{7,1},{8,10},{9,11},{10,... | collective-permute-start | bytes 786440 | tf_op jit(solution)/shard_map/ppermute | solution.py:179
  179.5 19.8 %copy-start.21 = (bf16[128,1024]{0,1:T(8,128)(2,1)S(1)}, bf16[128,1024]{0,1:T(8,128)(2,1)}, u32[]{:S(2)}) copy-start(bf16[128,1024]{0,1:T(8,128)(2,1)} %get-tuple-element.74) | copy-start | bytes 786436
  179.5 27.8 %collective-permute-start.6 = (bf16[128,1024]{0,1:T(8,128)(2,1)}, bf16[128,1024]{0,1:T(8,128)(2,1)S(1)}, u32[]{:S(2)}, u32[]{:S(2)}) collective-permute-start(bf16[128,1024]{0,1:T(8,128)(2,1)} %get-tuple-element.74), channel_id=1, source_target_pairs={{0,3},{1,4},{2,5},{3,6},{4,7},{5,0},{6,1},{7,2},{8,11},{9,12},{10,... | collective-permute-start | bytes 786440 | tf_op jit(solution)/shard_map/ppermute | solution.py:179
  180.7 29.1 %collective-permute-start.7 = (bf16[128,1024]{0,1:T(8,128)(2,1)}, bf16[128,1024]{0,1:T(8,128)(2,1)S(1)}, u32[]{:S(2)}, u32[]{:S(2)}) collective-permute-start(bf16[128,1024]{0,1:T(8,128)(2,1)} %get-tuple-element.74), channel_id=1, source_target_pairs={{0,4},{1,5},{2,6},{3,7},{4,0},{5,1},{6,2},{7,3},{8,12},{9,13},{10,... | collective-permute-start | bytes 786440 | tf_op jit(solution)/shard_map/ppermute | solution.py:179
  181.9 32.8 %collective-permute-start.8 = (bf16[128,1024]{0,1:T(8,128)(2,1)}, bf16[128,1024]{0,1:T(8,128)(2,1)S(1)}, u32[]{:S(2)}, u32[]{:S(2)}) collective-permute-start(bf16[128,1024]{0,1:T(8,128)(2,1)} %get-tuple-element.74), channel_id=1, source_target_pairs={{0,5},{1,6},{2,7},{3,0},{4,1},{5,2},{6,3},{7,4},{8,13},{9,14},{10,... | collective-permute-start | bytes 786440 | tf_op jit(solution)/shard_map/ppermute | solution.py:179
  194.2 22.9 %collective-permute-start.9 = (bf16[128,1024]{0,1:T(8,128)(2,1)}, bf16[128,1024]{0,1:T(8,128)(2,1)S(1)}, u32[]{:S(2)}, u32[]{:S(2)}) collective-permute-start(bf16[128,1024]{0,1:T(8,128)(2,1)} %get-tuple-element.74), channel_id=1, source_target_pairs={{0,6},{1,7},{2,0},{3,1},{4,2},{5,3},{6,4},{7,5},{8,14},{9,15},{10,... | collective-permute-start | bytes 786440 | tf_op jit(solution)/shard_map/ppermute | solution.py:179
  199.3 20.3 %collective-permute-start.10 = (bf16[128,1024]{0,1:T(8,128)(2,1)S(1)}, bf16[128,1024]{0,1:T(8,128)(2,1)S(1)}, u32[]{:S(2)}, u32[]{:S(2)}) collective-permute-start(bf16[128,1024]{0,1:T(8,128)(2,1)S(1)} %copy-done.21), channel_id=1, source_target_pairs={{0,7},{1,0},{2,1},{3,2},{4,3},{5,4},{6,5},{7,6},{8,15},{9,8},{10,9... | collective-permute-start | bytes 786440 | tf_op jit(solution)/shard_map/ppermute | solution.py:179
  231.2 3.2 %copy-start.18 = (bf16[128,1024]{0,1:T(8,128)(2,1)S(1)}, bf16[128,1024]{0,1:T(8,128)(2,1)}, u32[]{:S(2)}) copy-start(bf16[128,1024]{0,1:T(8,128)(2,1)} %reduce-scatter.2.cloned.1.call-done) | copy-start | bytes 786436
  231.2 3.5 %copy-start.19 = (bf16[128,8,128]{0,2,1:T(8,128)(2,1)S(1)}, bf16[128,8,128]{0,2,1:T(8,128)(2,1)}, u32[]{:S(2)}) copy-start(bf16[128,8,128]{0,2,1:T(8,128)(2,1)} %pad_maximum_fusion.2) | copy-start | bytes 786436
  240.3 7.3 %copy-start.2 = (bf16[128,1280]{1,0:T(8,128)(2,1)S(1)}, bf16[128,1280]{1,0:T(8,128)(2,1)}, u32[]{:S(2)}) copy-start(bf16[128,1280]{1,0:T(8,128)(2,1)} %copy-done.1) | copy-start | bytes 983044
  240.3 8.3 %copy-start.4 = (bf16[128,1280]{1,0:T(8,128)(2,1)S(1)}, bf16[128,1280]{1,0:T(8,128)(2,1)}, u32[]{:S(2)}) copy-start(bf16[128,1280]{1,0:T(8,128)(2,1)} %copy-done.3) | copy-start | bytes 983044
  240.3 9.2 %copy-start.6 = (bf16[128,1280]{1,0:T(8,128)(2,1)S(1)}, bf16[128,1280]{1,0:T(8,128)(2,1)}, u32[]{:S(2)}) copy-start(bf16[128,1280]{1,0:T(8,128)(2,1)} %copy-done.5) | copy-start | bytes 983044
  241.3 9.1 %copy-start.8 = (bf16[128,1280]{1,0:T(8,128)(2,1)S(1)}, bf16[128,1280]{1,0:T(8,128)(2,1)}, u32[]{:S(2)}) copy-start(bf16[128,1280]{1,0:T(8,128)(2,1)} %copy-done.7) | copy-start | bytes 983044
  242.1 9.2 %copy-start.10 = (bf16[128,1280]{1,0:T(8,128)(2,1)S(1)}, bf16[128,1280]{1,0:T(8,128)(2,1)}, u32[]{:S(2)}) copy-start(bf16[128,1280]{1,0:T(8,128)(2,1)} %copy-done.9) | copy-start | bytes 983044
  242.1 12.0 %collective-permute-start.11 = (bf16[4,128,256]{2,1,0:T(8,128)(2,1)}, bf16[4,128,256]{2,1,0:T(8,128)(2,1)}, u32[]{:S(2)}, u32[]{:S(2)}) collective-permute-start(bf16[4,128,256]{2,1,0:T(8,128)(2,1)} %bitcast.25), channel_id=1, source_target_pairs={{32,0},{40,8},{48,16},{56,24},{64,32},{72,40},{80,48},{88,56},{96,... | collective-permute-start | bytes 786440 | tf_op jit(solution)/shard_map/ppermute | solution.py:30
  244.4 7.9 %copy-start.12 = (bf16[128,1280]{1,0:T(8,128)(2,1)S(1)}, bf16[128,1280]{1,0:T(8,128)(2,1)}, u32[]{:S(2)}) copy-start(bf16[128,1280]{1,0:T(8,128)(2,1)} %copy-done.11) | copy-start | bytes 983044
  244.5 8.7 %copy-start.14 = (bf16[128,1280]{1,0:T(8,128)(2,1)S(1)}, bf16[128,1280]{1,0:T(8,128)(2,1)}, u32[]{:S(2)}) copy-start(bf16[128,1280]{1,0:T(8,128)(2,1)} %copy-done.13) | copy-start | bytes 983044
  244.5 14.3 %collective-permute-start.13 = (bf16[2,128,256]{2,1,0:T(8,128)(2,1)S(1)}, bf16[2,128,256]{2,1,0:T(8,128)(2,1)S(1)}, u32[]{:S(2)}, u32[]{:S(2)}) collective-permute-start(bf16[2,128,256]{2,1,0:T(8,128)(2,1)S(1)} %bitcast.197), channel_id=1, source_target_pairs={{64,0},{72,8},{80,16},{88,24},{96,32},{104,40},{112,48},{120,56},{... | collective-permute-start | bytes 393224 | tf_op jit(solution)/shard_map/ppermute | solution.py:30
  250.4 7.3 %copy-start.23 = (f32[128,64]{0,1:T(8,128)S(1)}, f32[128,64]{0,1:T(8,128)}, u32[]{:S(2)}) copy-start(f32[128,64]{0,1:T(8,128)} %copy-done.22) | copy-start | bytes 98308
  250.4 7.3 %copy-start.25 = (f32[128,64]{0,1:T(8,128)S(1)}, f32[128,64]{0,1:T(8,128)}, u32[]{:S(2)}) copy-start(f32[128,64]{0,1:T(8,128)} %get-tuple-element.38) | copy-start | bytes 98308
  255.2 21.3 %copy-start.27 = (f32[64]{0:T(128)S(1)}, f32[64]{0:T(128)}, u32[]{:S(2)}) copy-start(f32[64]{0:T(128)} %copy-done.26) | copy-start | bytes 772
  255.2 21.3 %copy-start.29 = (pred[64]{0:T(512)(128)(4,1)S(1)}, pred[64]{0:T(512)(128)(4,1)}, u32[]{:S(2)}) copy-start(pred[64]{0:T(512)(128)(4,1)} %copy-done.28) | copy-start | bytes 196
  255.2 21.3 %copy-start.31 = (pred[64]{0:T(512)(128)(4,1)S(1)}, pred[64]{0:T(512)(128)(4,1)}, u32[]{:S(2)}) copy-start(pred[64]{0:T(512)(128)(4,1)} %copy-done.30) | copy-start | bytes 196
  255.3 7.2 %collective-permute-start.12 = (bf16[2,128,256]{2,1,0:T(8,128)(2,1)S(1)}, bf16[2,128,256]{2,1,0:T(8,128)(2,1)S(1)}, u32[]{:S(2)}, u32[]{:S(2)}) collective-permute-start(bf16[2,128,256]{2,1,0:T(8,128)(2,1)S(1)} %slice.350), channel_id=1, source_target_pairs={{16,0},{24,8},{32,16},{40,24},{48,32},{56,40},{64,48},{72,56},{80,... | collective-permute-start | bytes 393224 | tf_op jit(solution)/shard_map/ppermute | solution.py:30
  262.5 13.3 %collective-permute-start.14 = (bf16[1,128,256]{2,1,0:T(8,128)(2,1)S(1)}, bf16[1,128,256]{2,1,0:T(8,128)(2,1)S(1)}, u32[]{:S(2)}, u32[]{:S(2)}) collective-permute-start(bf16[1,128,256]{2,1,0:T(8,128)(2,1)S(1)} %slice.351), channel_id=1, source_target_pairs={{8,0},{16,8},{24,16},{32,24},{40,32},{48,40},{56,48},{64,56},{72,6... | collective-permute-start | bytes 196616 | tf_op jit(solution)/shard_map/ppermute | solution.py:30
  (9 other events, 7.0 us)
Sparse Core Ops, SparseCore 0:
  10.8 148.0 all-gather.1
  170.7 60.5 reduce-scatter.1

commit v3 on v2

--- a/solution.py
+++ b/solution.py
@@ -126,13 +126,34 @@
         .astype(jnp.bfloat16)
         .reshape(length, groups * HD)
     )
-    w_cols = lax.all_gather(out_weight, SEQ, axis=1, tiled=True)
-    og_perm = out_grad
+    kv_count = lax.axis_size("kv")
+    kv_me = lax.axis_index("kv")
+    rows = queries.shape[1]
+    order = list(range(1, kv_count)) + [0]
+    chunk = 2 if kv_count % 2 == 0 else 1
+    w_parts = {}
+    for c in range(0, kv_count, chunk):
+        steps = order[c : c + chunk]
+        local = jnp.concatenate(
+            [
+                lax.dynamic_slice_in_dim(out_weight, ((kv_me + j) % kv_count) * rows, rows, 0)
+                for j in steps
+            ],
+            axis=0,
+        )
+        gathered = lax.all_gather(local, SEQ, axis=1, tiled=True)
+        for i, j in enumerate(steps):
+            w_parts[j] = gathered[i * rows : (i + 1) * rows]
     contract = (((1,), (1,)), ((), ()))
-    hg_part = lax.dot_general(og_perm, w_cols, contract, preferred_element_type=jnp.float32)
-    head_grad = lax.psum_scatter(
-        hg_part.astype(jnp.bfloat16), "kv", scatter_dimension=1, tiled=True
-    )
+    hg_sum = None
+    for j in order:
+        hg_j = lax.dot_general(
+            out_grad, w_parts[j], contract, preferred_element_type=jnp.float32
+        ).astype(jnp.bfloat16)
+        if j != 0:
+            hg_j = lax.ppermute(hg_j, "kv", [(i, (i + j) % kv_count) for i in range(kv_count)])
+        hg_sum = hg_j.astype(jnp.float32) if hg_sum is None else hg_sum + hg_j.astype(jnp.float32)
+    head_grad = hg_sum.astype(jnp.bfloat16)
     width = keys.shape[1]
     doc_row = jnp.zeros((1, 2 * width), jnp.bfloat16).at[0, :length].set(
         doc_ids.astype(jnp.bfloat16)
@@ -167,19 +188,12 @@
         dvalue_sum = dvalue_sum + dvalue
     attn = jnp.concatenate(outputs, axis=1)
     dq_rot = jnp.stack(dqueries, axis=1)
-    kv_count = lax.axis_size("kv")
-    kv_me = lax.axis_index("kv")
-    rows = attn.shape[1]
     total = None
-    for step in range(kv_count):
-        if step == 0:
-            piece = attn
-        else:
-            route = [(i, (i + step) % kv_count) for i in range(kv_count)]
-            piece = lax.ppermute(attn, "kv", route)
-        src = (kv_me - step) % kv_count
-        w_rows = lax.dynamic_slice_in_dim(w_cols, src * rows, rows, 0)
-        part = jnp.dot(piece, w_rows, preferred_element_type=jnp.float32).astype(jnp.bfloat16)
+    for j in order:
+        piece = attn
+        if j != 0:
+            piece = lax.ppermute(attn, "kv", [(i, (i - j) % kv_count) for i in range(kv_count)])
+        part = jnp.dot(piece, w_parts[j], preferred_element_type=jnp.float32).astype(jnp.bfloat16)
         part = lax.optimization_barrier(part)
         total = part.astype(jnp.float32) if total is None else total + part.astype(jnp.float32)
     layer_out = total.astype(jnp.bfloat16)

time: 288 us -> 465 us (1.61); the launches traced: 284 us -> 456 us
  waiting for transfers between devices: 134 us -> 305 us
  starting transfers between devices: 45.8 us -> 62.5 us
  matrix products: 64.5 us -> 54 us
  other arithmetic: 18.8 us -> 13.8 us
    all_gather x1 -> x4, waiting for transfers between devices: 88.3 us -> 275 us  [per_device(): gathered = lax.all_gather(local, SEQ, axis=1, tiled=True)]
    ppermute x7 -> x14, starting transfers between devices: 11.7 us -> 25.9 us  [the longest x7 15.3 us: per_device(): lax.ppermute(attn, 'kv', [(i, (i - j) % kv_count) for i in range(kv_count)])]
    ppermute x7 -> x14, waiting for transfers between devices: 17.1 us -> 10.3 us  [the longest x7 10.3 us: per_device(): lax.ppermute(hg_j, 'kv', [(i, (i + j) % kv_count) for i in range(kv_count)])]
    dot_general x8, matrix products: 10.8 us -> 4.14 us  [attend(): lax.dot_general(query, key_win, contract, preferred_element_type=jnp.floa...]
    reduce_scatter x1 -> x0, waiting for transfers between devices: 5.68 us -> none  [per_device(): lax.psum_scatter(hg_part.astype(jnp.bfloat16), 'kv', scatter_dimension=1,...]
    dot_general x9 -> x16, matrix products: 31.4 us -> 33.3 us  [the longest x8 21.1 us: per_device(): jnp.dot(piece, w_parts[j], preferred_element_type=jnp.float32)]
  transfers between devices with their start and end apart: 17 -> 26, of which waited for: 10 -> 12; matrix products, arithmetic and copies ran while one was open for 22% -> 13% of each run, Pallas kernels for 0% -> 0%
where the time goes in v3:
time: 465 us; the launch traced here: 456 us
  waiting for transfers between devices  305 us (66%)
  starting transfers between devices  62.5 us (13%)
  matrix products  54 us (12%)
  between operations  15.4 us (3%)
  other arithmetic  13.8 us (3%)
  local copies, waits for them, and re-layouts  4.91 us (1%)
    all_gather x4, waiting for transfers between devices, per_device(): gathered = lax.all_gather(local, SEQ, axis=1, tiled=True)  275 us
    ppermute x8, starting transfers between devices, shifted(): return lax.ppermute(block, SEQ, route)  36.5 us
    dot_general x8, matrix products, per_device(): jnp.dot(piece, w_parts[j], preferred_element_type=jnp.float32)  21.1 us
    ppermute x8, waiting for transfers between devices, shifted(): return lax.ppermute(block, SEQ, route)  20.1 us
    ppermute x7, starting transfers between devices, per_device(): lax.ppermute(attn, 'kv', [(i, (i - j) % kv_count) for i in range(kv_count)])  15.3 us
    dot_general x8, matrix products, per_device(): lax.dot_general(out_grad, w_parts[j], contract, preferred_element_type=jn...  12.1 us
    ppermute x7, starting transfers between devices, per_device(): lax.ppermute(hg_j, 'kv', [(i, (i + j) % kv_count) for i in range(kv_count)])  10.6 us
    ppermute x7, waiting for transfers between devices, per_device(): lax.ppermute(hg_j, 'kv', [(i, (i + j) % kv_count) for i in range(kv_count)])  10.3 us
  transfers between devices with their start and end apart: 26, of which 12 were waited for; matrix products, arithmetic and copies ran while one was open for 13% of the time, Pallas kernels for 0%

profile of v3, /device:TPU:97, one launch (start us, length us, event | category | flops | bytes accessed | tf_op | source)
XLA Modules:
  0.0 455.8 jit_solution(11459200922650909806)
XLA Ops:
  7.4 1.1 constant_dynamic-slice_fusion.7
  12.7 5.2 %collective-permute-start = (bf16[1,129,256]{2,1,0:T(8,128)(2,1)S(1)}, bf16[1,129,256]{2,1,0:T(8,128)(2,1)S(1)}, u32[]{:S(2)}, u32[]{:S(2)}) collective-permute-start(bf16[1,129,256]{2,1,0:T(8,128)(2,1)S(1)} %fusion.162), channel_id=1, source_target_pairs={{0,8},{8,16},{16,24},{24,32},{32,40},{40,48},{48,56},{56,64},{64,7... | collective-permute-start | bytes 198152 | tf_op jit(solution)/shard_map/ppermute | solution.py:30
  19.8 4.7 %collective-permute-start.2 = (bf16[2,129,256]{2,1,0:T(8,128)(2,1)S(1)}, bf16[2,129,256]{2,1,0:T(8,128)(2,1)S(1)}, u32[]{:S(2)}, u32[]{:S(2)}) collective-permute-start(bf16[2,129,256]{2,1,0:T(8,128)(2,1)S(1)} %pad_maximum_fusion.4), channel_id=1, source_target_pairs={{0,16},{8,24},{16,32},{24,40},{32,48},{40,56},{48,64},{56,72},{64,... | collective-permute-start | bytes 396296 | tf_op jit(solution)/shard_map/ppermute | solution.py:30
  24.6 3.1 collective-permute-start.1
  28.1 6.0 %collective-permute-start.3 = (bf16[4,129,256]{2,1,0:T(8,128)(2,1)S(1)}, bf16[4,129,256]{2,1,0:T(8,128)(2,1)S(1)}, u32[]{:S(2)}, u32[]{:S(2)}) collective-permute-start(bf16[4,129,256]{2,1,0:T(8,128)(2,1)S(1)} %pad_maximum_fusion.1), channel_id=1, source_target_pairs={{0,32},{8,40},{16,48},{24,56},{32,64},{40,72},{48,80},{56,88},{64,... | collective-permute-start | bytes 792584 | tf_op jit(solution)/shard_map/ppermute | solution.py:30
  34.6 8.3 %collective-permute-done.3 = bf16[4,129,256]{2,1,0:T(8,128)(2,1)S(1)} collective-permute-done((bf16[4,129,256]{2,1,0:T(8,128)(2,1)S(1)}, bf16[4,129,256]{2,1,0:T(8,128)(2,1)S(1)}, u32[]{:S(2)}, u32[]{:S(2)}) %collective-permute-start.3) | collective-permute-done | bytes 264224 | tf_op jit(solution)/shard_map/ppermute | solution.py:30
  51.9 0.9 constant_dynamic-update-slice_fusion.10
  53.1 0.9 constant_dynamic-update-slice_fusion.9
  54.3 0.9 constant_dynamic-update-slice_fusion.8
  56.6 0.9 constant_dynamic-update-slice_fusion.6
  58.7 1.0 collective-permute-start.10
  59.7 2.6 collective-permute-start.9
  62.3 3.3 collective-permute-start.8
  65.6 1.6 collective-permute-start.6
  67.2 39.9 %all-gather.11.cloned.1.call-done = bf16[2048,1024]{0,1:T(8,128)(2,1)} async-done(((bf16[2048,32]{0,1:T(8,128)(2,1)}), bf16[2048,1024]{0,1:T(8,128)(2,1)}) %all-gather.11.cloned.1.call-update) | async-done | bytes 4194320 | tf_op jit(solution)/shard_map/all_gather | solution.py:144
  107.1 3.2 fusion.100
  110.3 6.2 %collective-permute-start.5 = (bf16[128,1024]{0,1:T(8,128)(2,1)}, bf16[128,1024]{0,1:T(8,128)(2,1)}, u32[]{:S(2)}, u32[]{:S(2)}) collective-permute-start(bf16[128,1024]{0,1:T(8,128)(2,1)} %get-tuple-element.82), channel_id=1, source_target_pairs={{0,6},{1,7},{2,0},{3,1},{4,2},{5,3},{6,4},{7,5},{8,14},{9,15},{10,... | collective-permute-start | bytes 786440 | tf_op jit(solution)/shard_map/ppermute | solution.py:195
  116.5 3.2 fusion.94
  120.3 76.7 %all-gather.9.cloned.1.call-done = bf16[2048,1024]{0,1:T(8,128)(2,1)} async-done(((bf16[2048,32]{0,1:T(8,128)(2,1)}), bf16[2048,1024]{0,1:T(8,128)(2,1)}) %all-gather.9.cloned.1.call-update) | async-done | bytes 4194320 | tf_op jit(solution)/shard_map/all_gather | solution.py:144
  197.0 3.2 fusion.88
  200.2 83.0 %all-gather.5.cloned.1.call-done = bf16[2048,1024]{0,1:T(8,128)(2,1)} async-done(((bf16[2048,32]{0,1:T(8,128)(2,1)}), bf16[2048,1024]{0,1:T(8,128)(2,1)}) %all-gather.5.cloned.1.call-update) | async-done | bytes 4194320 | tf_op jit(solution)/shard_map/all_gather | solution.py:144
  283.2 3.2 fusion.127
  286.4 2.7 collective-permute-start.12
  289.1 3.2 fusion.82
  292.4 1.5 fusion.130
  294.1 75.1 %all-gather.7.cloned.1.call-done = bf16[2048,1024]{0,1:T(8,128)(2,1)} async-done(((bf16[2048,32]{0,1:T(8,128)(2,1)}), bf16[2048,1024]{0,1:T(8,128)(2,1)}) %all-gather.7.cloned.1.call-update) | async-done | bytes 4194320 | tf_op jit(solution)/shard_map/all_gather | solution.py:144
  369.2 2.6 fusion.76
  371.9 2.5 fusion.115
  374.4 2.8 collective-permute-start.16
  377.2 1.9 fusion.70
  380.0 1.5 collective-permute-start.15
  381.4 1.8 fusion.64
  384.4 1.9 fusion.58
  387.9 2.3 collective-permute-start.13
  390.8 1.1 add_convert_fusion.1
  392.0 3.8 collective-permute-done.14
  395.7 6.5 %collective-permute-done.13 = bf16[128,1024]{0,1:T(8,128)(2,1)S(1)} collective-permute-done((bf16[128,1024]{0,1:T(8,128)(2,1)S(1)}, bf16[128,1024]{0,1:T(8,128)(2,1)S(1)}, u32[]{:S(2)}, u32[]{:S(2)}) %collective-permute-start.13) | collective-permute-done | bytes 262176 | tf_op jit(solution)/shard_map/ppermute | solution.py:154
  402.3 1.9 add_convert_fusion
  414.1 1.9 collective-permute-start.18
  416.5 2.7 collective-permute-start.20
  419.2 0.9 fusion.134
  420.1 3.0 collective-permute-done.18
  423.1 1.0 convert_add_fusion
  424.1 2.4 collective-permute-start.19
  426.6 1.1 subtract_convert_fusion
  427.7 3.6 collective-permute-done.19
  431.4 10.5 %collective-permute-start.21 = (bf16[1,128,256]{2,1,0:T(8,128)(2,1)S(1)}, bf16[1,128,256]{2,1,0:T(8,128)(2,1)S(1)}, u32[]{:S(2)}, u32[]{:S(2)}) collective-permute-start(bf16[1,128,256]{2,1,0:T(8,128)(2,1)S(1)} %slice.473), channel_id=1, source_target_pairs={{8,0},{16,8},{24,16},{32,24},{40,32},{48,40},{56,48},{64,56},{72,6... | collective-permute-start | bytes 196616 | tf_op jit(solution)/shard_map/ppermute | solution.py:30
  442.8 4.4 collective-permute-done.21
  (214 shorter events, 36.4 us)
Async XLA Ops:
  7.2 276.0 %copy-start = (bf16[128,1024]{1,0:T(8,128)(2,1)S(1)}, bf16[128,1024]{1,0:T(8,128)(2,1)}, u32[]{:S(2)}) copy-start(bf16[128,1024]{1,0:T(8,128)(2,1)} %param.14) | copy-start | bytes 786436
  7.2 12.2 %copy-start.6 = (bf16[128,1024]{1,0:T(8,128)(2,1)S(1)}, bf16[128,1024]{1,0:T(8,128)(2,1)}, u32[]{:S(2)}) copy-start(bf16[128,1024]{1,0:T(8,128)(2,1)} %param.10) | copy-start | bytes 786436
  7.2 99.9 %all-gather.11.cloned.1.call-start = ((), (), s32[]{:S(2)}) async-start(), calls=%async_computation.3 | async-start | bytes 4325376 | tf_op jit(solution)/shard_map/all_gather | solution.py:144
  7.3 12.2 %copy-start.34 = (s32[1,32]{1,0:T(1,128)S(1)}, s32[1,32]{1,0:T(1,128)}, u32[]{:S(2)}) copy-start(s32[1,32]{1,0:T(1,128)} %param.16) | copy-start | bytes 388
  9.2 187.8 %all-gather.9.cloned.1.call-start = ((), (), s32[]{:S(2)}) async-start(), calls=%async_computation.2 | async-start | bytes 4325376 | tf_op jit(solution)/shard_map/all_gather | solution.py:144
  10.0 273.2 %all-gather.5.cloned.1.call-start = ((), (), s32[]{:S(2)}) async-start(), calls=%async_computation | async-start | bytes 4325376 | tf_op jit(solution)/shard_map/all_gather | solution.py:144
  10.7 358.5 %all-gather.7.cloned.1.call-start = ((), (), s32[]{:S(2)}) async-start(), calls=%async_computation.1 | async-start | bytes 4325376 | tf_op jit(solution)/shard_map/all_gather | solution.py:144
  11.4 8.2 %copy-start.22 = (f32[64]{0:T(128)}, f32[64]{0:T(128)S(1)}, u32[]{:S(2)}) copy-start(f32[64]{0:T(128)S(1)} %multiply_exponential_fusion) | copy-start | bytes 772
  11.5 8.2 %copy-start.24 = (pred[64]{0:T(512)(128)(4,1)}, pred[64]{0:T(512)(128)(4,1)S(1)}, u32[]{:S(2)}) copy-start(pred[64]{0:T(512)(128)(4,1)S(1)} %get-tuple-element.84) | copy-start | bytes 196
  11.5 8.2 %copy-start.26 = (pred[64]{0:T(512)(128)(4,1)}, pred[64]{0:T(512)(128)(4,1)S(1)}, u32[]{:S(2)}) copy-start(pred[64]{0:T(512)(128)(4,1)S(1)} %get-tuple-element.85) | copy-start | bytes 196
  12.7 7.2 %collective-permute-start = (bf16[1,129,256]{2,1,0:T(8,128)(2,1)S(1)}, bf16[1,129,256]{2,1,0:T(8,128)(2,1)S(1)}, u32[]{:S(2)}, u32[]{:S(2)}) collective-permute-start(bf16[1,129,256]{2,1,0:T(8,128)(2,1)S(1)} %fusion.162), channel_id=1, source_target_pairs={{0,8},{8,16},{16,24},{24,32},{32,40},{40,48},{48,56},{56,64},{64,7... | collective-permute-start | bytes 198152 | tf_op jit(solution)/shard_map/ppermute | solution.py:30
  19.4 14.7 %copy-start.4 = (f32[128,64]{0,1:T(8,128)}, f32[128,64]{0,1:T(8,128)S(1)}, u32[]{:S(2)}) copy-start(f32[128,64]{0,1:T(8,128)S(1)} %get-tuple-element.48) | copy-start | bytes 98308
  19.8 8.2 %collective-permute-start.2 = (bf16[2,129,256]{2,1,0:T(8,128)(2,1)S(1)}, bf16[2,129,256]{2,1,0:T(8,128)(2,1)S(1)}, u32[]{:S(2)}, u32[]{:S(2)}) collective-permute-start(bf16[2,129,256]{2,1,0:T(8,128)(2,1)S(1)} %pad_maximum_fusion.4), channel_id=1, source_target_pairs={{0,16},{8,24},{16,32},{24,40},{32,48},{40,56},{48,64},{56,72},{64,... | collective-permute-start | bytes 396296 | tf_op jit(solution)/shard_map/ppermute | solution.py:30
  24.6 10.0 %collective-permute-start.1 = (bf16[2,129,256]{2,1,0:T(8,128)(2,1)S(1)}, bf16[2,129,256]{2,1,0:T(8,128)(2,1)S(1)}, u32[]{:S(2)}, u32[]{:S(2)}) collective-permute-start(bf16[2,129,256]{2,1,0:T(8,128)(2,1)S(1)} %pad_maximum_fusion.4), channel_id=1, source_target_pairs={{0,64},{8,72},{16,80},{24,88},{32,96},{40,104},{48,112},{56,120},{... | collective-permute-start | bytes 396296 | tf_op jit(solution)/shard_map/ppermute | solution.py:30
  28.1 14.8 %collective-permute-start.3 = (bf16[4,129,256]{2,1,0:T(8,128)(2,1)S(1)}, bf16[4,129,256]{2,1,0:T(8,128)(2,1)S(1)}, u32[]{:S(2)}, u32[]{:S(2)}) collective-permute-start(bf16[4,129,256]{2,1,0:T(8,128)(2,1)S(1)} %pad_maximum_fusion.1), channel_id=1, source_target_pairs={{0,32},{8,40},{16,48},{24,56},{32,64},{40,72},{48,80},{56,88},{64,... | collective-permute-start | bytes 792584 | tf_op jit(solution)/shard_map/ppermute | solution.py:30
  34.1 14.5 %copy-start.1 = (bf16[128,8,128]{0,2,1:T(8,128)(2,1)}, bf16[128,8,128]{0,2,1:T(8,128)(2,1)S(1)}, u32[]{:S(2)}) copy-start(bf16[128,8,128]{0,2,1:T(8,128)(2,1)S(1)} %pad_maximum_fusion.2) | copy-start | bytes 786436
  58.7 51.6 %collective-permute-start.10 = (bf16[128,1024]{0,1:T(8,128)(2,1)}, bf16[128,1024]{0,1:T(8,128)(2,1)}, u32[]{:S(2)}, u32[]{:S(2)}) collective-permute-start(bf16[128,1024]{0,1:T(8,128)(2,1)} %get-tuple-element.82), channel_id=1, source_target_pairs={{0,1},{1,2},{2,3},{3,4},{4,5},{5,6},{6,7},{7,0},{8,9},{9,10},{10,1... | collective-permute-start | bytes 786440 | tf_op jit(solution)/shard_map/ppermute | solution.py:195
  59.7 60.1 %collective-permute-start.9 = (bf16[128,1024]{0,1:T(8,128)(2,1)}, bf16[128,1024]{0,1:T(8,128)(2,1)}, u32[]{:S(2)}, u32[]{:S(2)}) collective-permute-start(bf16[128,1024]{0,1:T(8,128)(2,1)} %get-tuple-element.82), channel_id=1, source_target_pairs={{0,2},{1,3},{2,4},{3,5},{4,6},{5,7},{6,0},{7,1},{8,10},{9,11},{10,... | collective-permute-start | bytes 786440 | tf_op jit(solution)/shard_map/ppermute | solution.py:195
  62.3 224.1 %collective-permute-start.8 = (bf16[128,1024]{0,1:T(8,128)(2,1)}, bf16[128,1024]{0,1:T(8,128)(2,1)}, u32[]{:S(2)}, u32[]{:S(2)}) collective-permute-start(bf16[128,1024]{0,1:T(8,128)(2,1)} %get-tuple-element.82), channel_id=1, source_target_pairs={{0,3},{1,4},{2,5},{3,6},{4,7},{5,0},{6,1},{7,2},{8,11},{9,12},{10,... | collective-permute-start | bytes 786440 | tf_op jit(solution)/shard_map/ppermute | solution.py:195
  65.6 228.3 %collective-permute-start.7 = (bf16[128,1024]{0,1:T(8,128)(2,1)}, bf16[128,1024]{0,1:T(8,128)(2,1)}, u32[]{:S(2)}, u32[]{:S(2)}) collective-permute-start(bf16[128,1024]{0,1:T(8,128)(2,1)} %get-tuple-element.82), channel_id=1, source_target_pairs={{0,4},{1,5},{2,6},{3,7},{4,0},{5,1},{6,2},{7,3},{8,12},{9,13},{10,... | collective-permute-start | bytes 786440 | tf_op jit(solution)/shard_map/ppermute | solution.py:195
  65.6 308.8 %collective-permute-start.6 = (bf16[128,1024]{0,1:T(8,128)(2,1)}, bf16[128,1024]{0,1:T(8,128)(2,1)}, u32[]{:S(2)}, u32[]{:S(2)}) collective-permute-start(bf16[128,1024]{0,1:T(8,128)(2,1)} %get-tuple-element.82), channel_id=1, source_target_pairs={{0,5},{1,6},{2,7},{3,0},{4,1},{5,2},{6,3},{7,4},{8,13},{9,14},{10,... | collective-permute-start | bytes 786440 | tf_op jit(solution)/shard_map/ppermute | solution.py:195
  110.3 269.6 %collective-permute-start.5 = (bf16[128,1024]{0,1:T(8,128)(2,1)}, bf16[128,1024]{0,1:T(8,128)(2,1)}, u32[]{:S(2)}, u32[]{:S(2)}) collective-permute-start(bf16[128,1024]{0,1:T(8,128)(2,1)} %get-tuple-element.82), channel_id=1, source_target_pairs={{0,6},{1,7},{2,0},{3,1},{4,2},{5,3},{6,4},{7,5},{8,14},{9,15},{10,... | collective-permute-start | bytes 786440 | tf_op jit(solution)/shard_map/ppermute | solution.py:195
  119.7 264.3 %collective-permute-start.4 = (bf16[128,1024]{0,1:T(8,128)(2,1)}, bf16[128,1024]{0,1:T(8,128)(2,1)}, u32[]{:S(2)}, u32[]{:S(2)}) collective-permute-start(bf16[128,1024]{0,1:T(8,128)(2,1)} %get-tuple-element.82), channel_id=1, source_target_pairs={{0,7},{1,0},{2,1},{3,2},{4,3},{5,4},{6,5},{7,6},{8,15},{9,8},{10,9... | collective-permute-start | bytes 786440 | tf_op jit(solution)/shard_map/ppermute | solution.py:195
  283.2 9.2 %copy-start.30 = (bf16[2048,1024]{0,1:T(8,128)(2,1)S(1)}, bf16[2048,1024]{0,1:T(8,128)(2,1)}, u32[]{:S(2)}) copy-start(bf16[2048,1024]{0,1:T(8,128)(2,1)} %all-gather.5.cloned.1.call-done) | copy-start | bytes 12582916
  286.4 101.5 %collective-permute-start.12 = (bf16[128,1024]{0,1:T(8,128)(2,1)}, bf16[128,1024]{0,1:T(8,128)(2,1)}, u32[]{:S(2)}, u32[]{:S(2)}) collective-permute-start(bf16[128,1024]{0,1:T(8,128)(2,1)} %fusion.127), channel_id=1, source_target_pairs={{0,2},{1,3},{2,4},{3,5},{4,6},{5,7},{6,0},{7,1},{8,10},{9,11},{10,... | collective-permute-start | bytes 786440 | tf_op jit(solution)/shard_map/ppermute | solution.py:154
  293.8 96.4 %collective-permute-start.11 = (bf16[128,1024]{0,1:T(8,128)(2,1)}, bf16[128,1024]{0,1:T(8,128)(2,1)}, u32[]{:S(2)}, u32[]{:S(2)}) collective-permute-start(bf16[128,1024]{0,1:T(8,128)(2,1)} %fusion.130), channel_id=1, source_target_pairs={{0,1},{1,2},{2,3},{3,4},{4,5},{5,6},{6,7},{7,0},{8,9},{9,10},{10,1... | collective-permute-start | bytes 786440 | tf_op jit(solution)/shard_map/ppermute | solution.py:154
  374.4 17.5 %collective-permute-start.16 = (bf16[128,1024]{0,1:T(8,128)(2,1)S(1)}, bf16[128,1024]{0,1:T(8,128)(2,1)S(1)}, u32[]{:S(2)}, u32[]{:S(2)}) collective-permute-start(bf16[128,1024]{0,1:T(8,128)(2,1)S(1)} %fusion.115), channel_id=1, source_target_pairs={{0,6},{1,7},{2,0},{3,1},{4,2},{5,3},{6,4},{7,5},{8,14},{9,15},{10,... | collective-permute-start | bytes 786440 | tf_op jit(solution)/shard_map/ppermute | solution.py:154
  380.0 12.0 %collective-permute-start.15 = (bf16[128,1024]{0,1:T(8,128)(2,1)S(1)}, bf16[128,1024]{0,1:T(8,128)(2,1)S(1)}, u32[]{:S(2)}, u32[]{:S(2)}) collective-permute-start(bf16[128,1024]{0,1:T(8,128)(2,1)S(1)} %fusion.118), channel_id=1, source_target_pairs={{0,5},{1,6},{2,7},{3,0},{4,1},{5,2},{6,3},{7,4},{8,13},{9,14},{10,... | collective-permute-start | bytes 786440 | tf_op jit(solution)/shard_map/ppermute | solution.py:154
  384.0 11.7 %collective-permute-start.14 = (bf16[128,1024]{0,1:T(8,128)(2,1)S(1)}, bf16[128,1024]{0,1:T(8,128)(2,1)S(1)}, u32[]{:S(2)}, u32[]{:S(2)}) collective-permute-start(bf16[128,1024]{0,1:T(8,128)(2,1)S(1)} %fusion.121), channel_id=1, source_target_pairs={{0,4},{1,5},{2,6},{3,7},{4,0},{5,1},{6,2},{7,3},{8,12},{9,13},{10,... | collective-permute-start | bytes 786440 | tf_op jit(solution)/shard_map/ppermute | solution.py:154
  387.9 14.3 %collective-permute-start.13 = (bf16[128,1024]{0,1:T(8,128)(2,1)S(1)}, bf16[128,1024]{0,1:T(8,128)(2,1)S(1)}, u32[]{:S(2)}, u32[]{:S(2)}) collective-permute-start(bf16[128,1024]{0,1:T(8,128)(2,1)S(1)} %fusion.124), channel_id=1, source_target_pairs={{0,3},{1,4},{2,5},{3,6},{4,7},{5,0},{6,1},{7,2},{8,11},{9,12},{10,... | collective-permute-start | bytes 786440 | tf_op jit(solution)/shard_map/ppermute | solution.py:154
  390.3 12.0 %collective-permute-start.17 = (bf16[128,1024]{0,1:T(8,128)(2,1)S(1)}, bf16[128,1024]{0,1:T(8,128)(2,1)S(1)}, u32[]{:S(2)}, u32[]{:S(2)}) collective-permute-start(bf16[128,1024]{0,1:T(8,128)(2,1)S(1)} %fusion.112), channel_id=1, source_target_pairs={{0,7},{1,0},{2,1},{3,2},{4,3},{5,4},{6,5},{7,6},{8,15},{9,8},{10,9... | collective-permute-start | bytes 786440 | tf_op jit(solution)/shard_map/ppermute | solution.py:154
  391.9 12.5 %copy-start.11 = (bf16[128,128]{0,1:T(8,128)(2,1)S(1)}, bf16[128,128]{0,1:T(8,128)(2,1)}, u32[]{:S(2)}) copy-start(bf16[128,128]{0,1:T(8,128)(2,1)} %get-tuple-element.55) | copy-start | bytes 98308
  391.9 12.5 %copy-start.12 = (bf16[128,128]{0,1:T(8,128)(2,1)S(1)}, bf16[128,128]{0,1:T(8,128)(2,1)}, u32[]{:S(2)}) copy-start(bf16[128,128]{0,1:T(8,128)(2,1)} %get-tuple-element.59) | copy-start | bytes 98308
  391.9 12.5 %copy-start.13 = (bf16[128,128]{0,1:T(8,128)(2,1)S(1)}, bf16[128,128]{0,1:T(8,128)(2,1)}, u32[]{:S(2)}) copy-start(bf16[128,128]{0,1:T(8,128)(2,1)} %get-tuple-element.63) | copy-start | bytes 98308
  391.9 12.5 %copy-start.14 = (bf16[128,128]{0,1:T(8,128)(2,1)S(1)}, bf16[128,128]{0,1:T(8,128)(2,1)}, u32[]{:S(2)}) copy-start(bf16[128,128]{0,1:T(8,128)(2,1)} %get-tuple-element.67) | copy-start | bytes 98308
  391.9 12.5 %copy-start.15 = (bf16[128,128]{0,1:T(8,128)(2,1)S(1)}, bf16[128,128]{0,1:T(8,128)(2,1)}, u32[]{:S(2)}) copy-start(bf16[128,128]{0,1:T(8,128)(2,1)} %get-tuple-element.71) | copy-start | bytes 98308
  391.9 12.5 %copy-start.16 = (bf16[128,128]{0,1:T(8,128)(2,1)S(1)}, bf16[128,128]{0,1:T(8,128)(2,1)}, u32[]{:S(2)}) copy-start(bf16[128,128]{0,1:T(8,128)(2,1)} %get-tuple-element.75) | copy-start | bytes 98308
  391.9 12.5 %copy-start.17 = (bf16[128,128]{0,1:T(8,128)(2,1)S(1)}, bf16[128,128]{0,1:T(8,128)(2,1)}, u32[]{:S(2)}) copy-start(bf16[128,128]{0,1:T(8,128)(2,1)} %get-tuple-element.79) | copy-start | bytes 98308
  391.9 12.5 %copy-start.18 = (bf16[128,128]{0,1:T(8,128)(2,1)S(1)}, bf16[128,128]{0,1:T(8,128)(2,1)}, u32[]{:S(2)}) copy-start(bf16[128,128]{0,1:T(8,128)(2,1)} %get-tuple-element.83) | copy-start | bytes 98308
  414.1 8.9 %collective-permute-start.18 = (bf16[4,128,256]{2,1,0:T(8,128)(2,1)}, bf16[4,128,256]{2,1,0:T(8,128)(2,1)}, u32[]{:S(2)}, u32[]{:S(2)}) collective-permute-start(bf16[4,128,256]{2,1,0:T(8,128)(2,1)} %bitcast.33), channel_id=1, source_target_pairs={{32,0},{40,8},{48,16},{56,24},{64,32},{72,40},{80,48},{88,56},{96,... | collective-permute-start | bytes 786440 | tf_op jit(solution)/shard_map/ppermute | solution.py:30
  416.1 10.4 %copy-start.5 = (f32[128,64]{0,1:T(8,128)S(1)}, f32[128,64]{0,1:T(8,128)}, u32[]{:S(2)}) copy-start(f32[128,64]{0,1:T(8,128)} %copy-done.4) | copy-start | bytes 98308
  416.1 10.4 %copy-start.20 = (f32[128,64]{0,1:T(8,128)S(1)}, f32[128,64]{0,1:T(8,128)}, u32[]{:S(2)}) copy-start(f32[128,64]{0,1:T(8,128)} %get-tuple-element.46) | copy-start | bytes 98308
  416.5 11.2 %collective-permute-start.20 = (bf16[2,128,256]{2,1,0:T(8,128)(2,1)S(1)}, bf16[2,128,256]{2,1,0:T(8,128)(2,1)S(1)}, u32[]{:S(2)}, u32[]{:S(2)}) collective-permute-start(bf16[2,128,256]{2,1,0:T(8,128)(2,1)S(1)} %bitcast.219), channel_id=1, source_target_pairs={{64,0},{72,8},{80,16},{88,24},{96,32},{104,40},{112,48},{120,56},{... | collective-permute-start | bytes 393224 | tf_op jit(solution)/shard_map/ppermute | solution.py:30
  424.1 23.7 %copy-start.23 = (f32[64]{0:T(128)S(1)}, f32[64]{0:T(128)}, u32[]{:S(2)}) copy-start(f32[64]{0:T(128)} %copy-done.22) | copy-start | bytes 772
  424.1 23.7 %copy-start.25 = (pred[64]{0:T(512)(128)(4,1)S(1)}, pred[64]{0:T(512)(128)(4,1)}, u32[]{:S(2)}) copy-start(pred[64]{0:T(512)(128)(4,1)} %copy-done.24) | copy-start | bytes 196
  424.1 23.7 %copy-start.27 = (pred[64]{0:T(512)(128)(4,1)S(1)}, pred[64]{0:T(512)(128)(4,1)}, u32[]{:S(2)}) copy-start(pred[64]{0:T(512)(128)(4,1)} %copy-done.26) | copy-start | bytes 196
  424.1 7.2 %collective-permute-start.19 = (bf16[2,128,256]{2,1,0:T(8,128)(2,1)S(1)}, bf16[2,128,256]{2,1,0:T(8,128)(2,1)S(1)}, u32[]{:S(2)}, u32[]{:S(2)}) collective-permute-start(bf16[2,128,256]{2,1,0:T(8,128)(2,1)S(1)} %slice.472), channel_id=1, source_target_pairs={{16,0},{24,8},{32,16},{40,24},{48,32},{56,40},{64,48},{72,56},{80,... | collective-permute-start | bytes 393224 | tf_op jit(solution)/shard_map/ppermute | solution.py:30
  431.4 15.8 %collective-permute-start.21 = (bf16[1,128,256]{2,1,0:T(8,128)(2,1)S(1)}, bf16[1,128,256]{2,1,0:T(8,128)(2,1)S(1)}, u32[]{:S(2)}, u32[]{:S(2)}) collective-permute-start(bf16[1,128,256]{2,1,0:T(8,128)(2,1)S(1)} %slice.473), channel_id=1, source_target_pairs={{8,0},{16,8},{24,16},{32,24},{40,32},{48,40},{56,48},{64,56},{72,6... | collective-permute-start | bytes 196616 | tf_op jit(solution)/shard_map/ppermute | solution.py:30
  (14 other events, 57.4 us)
Sparse Core Ops, SparseCore 0:
  11.4 95.6 all-gather.10
  109.9 87.0 all-gather.8
  199.8 83.3 all-gather.4
  285.8 83.3 all-gather.6
